TPU v7x, 32 devices: a whole 2x2x4 slice. The times are simulated.
32 devices in a mesh: gx: 16 (over z, y, x), gy: 2 (over core).
Axes of the slice: x: 2, y: 2, z: 4, core: 2. Of those that a mesh axis runs over, the one named last changes fastest.
Arguments:
- coarse_state: float32 [24, 256, 256], P(None, 'gx', 'gy'), may hold values from -6 to 6
- coarse_rate: float32 [256, 256], P('gx', 'gy'), may hold values from 0.5 to 2
- fine_state: float32 [128, 24, 16, 256], P(('gx', 'gy')), may hold values from -6 to 6
- fine_rate: float32 [128, 16, 256], P(('gx', 'gy')), may hold values from 0.5 to 2
- refine_to: int32 [128], P(('gx', 'gy')), may hold values from -1 to 3, as said below
- parent_of: int32 [128], P(('gx', 'gy')), may hold values from -1 to 3, as said below
- kappa: float32 [24], replicated, may hold values from 0.01 to 0.05
- reaction: float32 [24, 24], replicated, may hold values from -1.25 to 1.25
Outputs:
- coarse_out: float32 [24, 256, 256], P(None, 'gx', 'gy')
- fine_out: float32 [128, 24, 16, 256], P(('gx', 'gy'))
Inputs may be any that keep to these rules, and one draw needn't show every extreme that they name: `refine_to`: -1 for a parent that is not refined; else k, the slot of its fine patch on the device k // 2 places higher along gx (wrapping), same gy index; no two parents name the same slot. `parent_of`: -1 for an empty slot; else p, its parent on the device k // 2 places lower along gx (wrapping), same gy index, k being the slot within its device; the two maps are inverse to each other; a device holds up to 4 live slots and in every draw some device holds that many.
All inputs are finite; a program needn't handle non-finite values.
Results may differ from a plain program's by a relative error of at most 0.0003.
Values sent between devices are 32-bit elements; how exact they have to be, the bound alone decides.
A program may use at most 64 MiB of HBM per device.

v0:
```python
import functools
import jax
import jax.numpy as jnp
from jax import lax
from jax.experimental import pallas as pl
from jax.experimental.pallas import tpu as pltpu
from jax.sharding import PartitionSpec as P

MESH = pl.DeviceIdType.MESH
F32 = jnp.float32
BF16 = jnp.bfloat16


def lanes(rows):
    return lax.broadcasted_iota(jnp.int32, (rows, 128), 1)


def pick(table, index):
    return jnp.take_along_axis(table, index, axis=1)


def powers(reaction, fields):
    row = lax.broadcasted_iota(jnp.int32, (fields, 3 * fields), 0)
    col = lax.broadcasted_iota(jnp.int32, (fields, 3 * fields), 1)
    power = (col % fields == row).astype(F32)
    result = []
    for _ in range(4):
        power = jnp.dot(
            reaction, power, precision=lax.Precision.HIGHEST, preferred_element_type=F32
        )
        result.append(power)
    return result, col < 2 * fields


def chem_weights(power_list, high_part, step):
    parts = []
    for count, (choose, power) in enumerate(zip((4.0, 6.0, 4.0, 1.0), power_list)):
        value = power * (choose * step ** (count + 1))
        high = value.astype(BF16).astype(F32)
        parts.append(jnp.where(high_part, high, value - high))
    return jnp.concatenate(parts, axis=0).astype(BF16)


def chemistry(weights, values, rates, fields):
    wide = jnp.concatenate(values, axis=1)
    high = wide.astype(BF16).astype(F32)
    low = wide - high
    stacked = jnp.concatenate([high, low, high], axis=0).astype(BF16)
    product = jnp.dot(weights, stacked, preferred_element_type=F32)
    out = []
    for n, (value, rate) in enumerate(zip(values, rates)):
        part = [
            product[q * fields : (q + 1) * fields, n * 128 : (n + 1) * 128] for q in range(4)
        ]
        rate = jnp.broadcast_to(rate, value.shape)
        out.append(value + rate * (part[0] + rate * (part[1] + rate * (part[2] + rate * part[3]))))
    return out


def kernel(
    n_gx, n_gy, fields, size_x, slots,
    refine_ref, parent_ref, coarse_hbm, crate_hbm, fine_hbm, frate_hbm, kappa_ref, reaction_ref,
    coarse_out_hbm, fine_out_hbm,
    cin, crate, fin, frate, fout, cout,
    buf_a, buf_b, row_send, col_send, hx, hy, cnew, cols, ring_local, ring_send, ring_recv,
    means, mean_send, mean_recv, wf_ref, wc_ref, rate8, edge_rate,
    in_sem, out_sem, send_sem, recv_sem,
):
    F = fields
    fine_cols = frate.shape[2]
    gx = lax.axis_index("gx")
    gy = lax.axis_index("gy")
    right = lax.rem(gx + 1, n_gx)
    left = lax.rem(gx + n_gx - 1, n_gx)
    above = lax.rem(gy + 1, n_gy)
    below = lax.rem(gy + n_gy - 1, n_gy)

    loads = [
        pltpu.make_async_copy(coarse_hbm, cin, in_sem.at[0]),
        pltpu.make_async_copy(crate_hbm, crate, in_sem.at[1]),
        pltpu.make_async_copy(frate_hbm, frate, in_sem.at[2]),
    ]
    fine_loads = []
    for s in range(slots):
        for h in range(2):
            fine_loads.append(
                pltpu.make_async_copy(
                    fine_hbm.at[s, :, pl.ds(h * 128, 128)], fin.at[s, h], in_sem.at[3 + 2 * s + h]
                )
            )
    for copy in loads + fine_loads:
        copy.start()

    barrier = pltpu.get_barrier_semaphore()
    for target in ((left, gy), (right, gy), (gx, below), (gx, above)):
        pl.semaphore_signal(barrier, inc=1, device_id=target, device_id_type=MESH)

    def send(n, src, dst, target):
        copy = pltpu.make_async_remote_copy(
            src_ref=src, dst_ref=dst, send_sem=send_sem.at[n], recv_sem=recv_sem.at[n],
            device_id=target, device_id_type=MESH,
        )
        copy.start()
        return copy

    lane = lanes(F)
    first_half = lane < 64

    def pack(rows_of, y):
        total = jnp.zeros((F, 128), F32)
        for x in range(size_x):
            shift = ((x - y) * 8) % 128
            row = rows_of(x)
            moved = pltpu.roll(row, shift, 1) if shift else row
            total = jnp.where(lane // 8 == x, moved, total)
        return total

    def halos(level):
        base = 4 * level
        return [
            send(base + 0, row_send.at[level, 1], hx.at[level, 0], (right, gy)),
            send(base + 1, row_send.at[level, 0], hx.at[level, 1], (left, gy)),
            send(base + 2, col_send.at[level, 1], hy.at[level, 0], (gx, above)),
            send(base + 3, col_send.at[level, 0], hy.at[level, 1], (gx, below)),
        ]

    loads[0].wait()
    old_rows = lambda x: cin[pl.ds(x, F, stride=size_x), :]
    row_send[0, 0] = old_rows(0)
    row_send[0, 1] = old_rows(size_x - 1)
    col_send[0, 0] = pack(old_rows, 0)
    col_send[0, 1] = pack(old_rows, size_x - 1)

    cols[0, 0] = pack(old_rows, size_x // 2 - 1)
    cols[0, 1] = pack(old_rows, size_x // 2)
    power_list, high_part = powers(reaction_ref[...], F)
    wf_ref[...] = chem_weights(power_list, high_part, 0.125)
    wc_ref[...] = chem_weights(power_list, high_part, 0.25)
    diag = lax.broadcasted_iota(jnp.int32, (F, F), 0) == lax.broadcasted_iota(jnp.int32, (F, F), 1)
    kappa_col = jnp.sum(
        jnp.where(diag, jnp.broadcast_to(kappa_ref[...], (F, F)), 0.0), axis=1, keepdims=True
    )
    kappa = jnp.broadcast_to(kappa_col, (F, 128))
    kappa2 = 2.0 * kappa

    for copy in fine_loads:
        copy.wait()
    for s in range(slots):
        for h in range(2):
            for x in range(size_x):
                buf_a[s, x + 1, :, pl.ds(h * 128, 128)] = fin[s, h, pl.ds(x, F, stride=size_x), :]
    loads[1].wait()
    loads[2].wait()
    for s in range(slots):
        for x in range(size_x):
            rate8[s, x] = jnp.broadcast_to(frate[s, pl.ds(x, 1), :], rate8.shape[2:])
    lane8 = lanes(8)
    for s in range(slots):
        for q in range(size_x // 4):
            total = jnp.zeros((8, 128), F32)
            for n in range(4):
                lo = rate8[s, 4 * q + n, :, pl.ds(0, 128)]
                hi = rate8[s, 4 * q + n, :, pl.ds(fine_cols - 128, 128)]
                lo = pltpu.roll(lo, 16 * n, 1) if n else lo
                shift = (16 * n - 48) % 128
                hi = pltpu.roll(hi, shift, 1) if shift else hi
                total = jnp.where(lane8 // 16 == n, lo, total)
                total = jnp.where(lane8 // 16 == 4 + n, hi, total)
            edge_rate[s, q] = total
    z16 = lane % 16
    row_index = (lane // 32) * 8 + z16 // 2
    col_index = jnp.where(lane < 64, 0, 64) + z16 // 2
    target = lane % 64
    mean_index = ((target // 8) % 4) * 32 + 2 * (target % 8)
    mean_low = target // 32 == 0

    def ring_of(level, s, side):
        return ring_local[level, s, side] if s < 2 else ring_recv[level, s - 2, side]

    def fine_step(s, step):
        src = buf_a if step == 0 else buf_b
        if step == 0:
            src[s, 0] = jnp.zeros((F, fine_cols), F32)
            src[s, size_x + 1] = jnp.zeros((F, fine_cols), F32)
        else:
            edge_x = 0.5 * (ring_of(0, s, 0) + ring_of(1, s, 0))
            edge_y = 0.5 * (ring_of(0, s, 1) + ring_of(1, s, 1))
            for h in range(2):
                src[s, 0, :, pl.ds(h * 128, 128)] = pick(edge_x, row_index + 32 * h)
                src[s, size_x + 1, :, pl.ds(h * 128, 128)] = pick(edge_x, row_index + 64 + 32 * h)
        weights = wf_ref[...]
        live = jnp.full((F, 128), parent_ref[s], jnp.int32) >= 0

        def pair(j, carry):
            ghost = pick(edge_y, col_index + 8 * j) if step else jnp.zeros((F, 128), F32)
            values, rates = [], []
            for n in range(2):
                x = 2 * j + n
                c = [src[s, x + 1, :, pl.ds(h * 128, 128)] for h in range(2)]
                up = [src[s, x, :, pl.ds(h * 128, 128)] for h in range(2)]
                dn = [src[s, x + 2, :, pl.ds(h * 128, 128)] for h in range(2)]
                ra = [pltpu.roll(v, 16, 1) for v in c]
                rb = [pltpu.roll(v, 112, 1) for v in c]
                yl = [jnp.where(lane < 16, ghost, ra[0]), jnp.where(lane < 16, ra[0], ra[1])]
                yh = [jnp.where(lane >= 112, rb[1], rb[0]), jnp.where(lane >= 112, ghost, rb[1])]
                for h in range(2):
                    v = c[h]
                    zl = jnp.where(z16 == 0, pltpu.roll(v, 113, 1), pltpu.roll(v, 1, 1))
                    zu = jnp.where(z16 == 15, pltpu.roll(v, 15, 1), pltpu.roll(v, 127, 1))
                    lap = (yl[h] + yh[h]) + (up[h] + dn[h]) + (zl + zu) - 6.0 * v
                    values.append(v + kappa2 * lap - 0.25 * (v - zl))
                    rate = rate8[s, x, :, pl.ds(h * 128, 128)]
                    rates.append(jnp.concatenate([rate] * (F // 8), axis=0))
            new = chemistry(weights, values, rates, F)
            if step == 0:
                for n in range(2):
                    for h in range(2):
                        buf_b[s, 2 * j + n + 1, :, pl.ds(h * 128, 128)] = new[2 * n + h]
            else:
                new = [jnp.where(live, v, 0.0) for v in new]
                for n in range(2):
                    for h in range(2):
                        fout[s, h, pl.ds(2 * j + n, F, stride=size_x), :] = new[2 * n + h]
                picked = []
                for h in range(2):
                    total = new[h] + new[2 + h]
                    total = total + pltpu.roll(total, 127, 1)
                    total = total + pltpu.roll(total, 112, 1)
                    picked.append(pick(total, mean_index))
                means[s, j] = 0.125 * jnp.where(mean_low, picked[0], picked[1])
            return carry

        lax.fori_loop(0, size_x // 2, pair, 0, unroll=4)

    edge_index = (lane // 64) * 64 + ((lane % 64) // 32) * 8 + z16 // 2

    def wide_rate(rate):
        return jnp.concatenate([rate] * (F // 8), axis=0)

    def correct(s):
        edge_x, edge_y = ring_of(0, s, 0), ring_of(0, s, 1)
        values, rates = [], []
        for side, x in ((0, 0), (1, size_x - 1)):
            for h in range(2):
                values.append(kappa2 * pick(edge_x, row_index + 64 * side + 32 * h))
                rates.append(wide_rate(rate8[s, x, :, pl.ds(h * 128, 128)]))
        for q in range(size_x // 4):
            values.append(kappa2 * pick(edge_y, edge_index + 16 * q))
            rates.append(wide_rate(edge_rate[s, q]))
        share = chemistry(wf_ref[...], values, rates, F)
        for x in range(size_x):
            q, n = x // 4, x % 4
            both = share[4 + q]
            lo = pltpu.roll(both, (-16 * n) % 128, 1) if n else both
            shift = (48 - 16 * n) % 128
            hi = pltpu.roll(both, shift, 1) if shift else both
            added = [jnp.where(lane < 16, lo, 0.0), jnp.where(lane >= 112, hi, 0.0)]
            for h in range(2):
                if x == 0:
                    added[h] = added[h] + share[h]
                if x == size_x - 1:
                    added[h] = added[h] + share[2 + h]
                here = (s, x + 1, slice(None), pl.ds(h * 128, 128))
                buf_b[here] = buf_b[here] + added[h]

    for s in ():
        fine_step(s, 0)
    pl.semaphore_wait(barrier, 4)
    old_halos = halos(0)
    for s in (0, 1):
        fine_step(s, 0)
    for copy in old_halos:
        copy.wait_recv()

    z8 = lane % 8
    for group in range(size_x // 4):
        values, rates = [], []
        for x in range(4 * group, 4 * group + 4):
            c = old_rows(x)
            up = old_rows(x - 1) if x > 0 else hx[0, 0]
            dn = old_rows(x + 1) if x < size_x - 1 else hx[0, 1]
            ghost_lo = pltpu.roll(hy[0, 0], (-x * 8) % 128, 1) if x else hy[0, 0]
            shift = (120 - x * 8) % 128
            ghost_hi = pltpu.roll(hy[0, 1], shift, 1) if shift else hy[0, 1]
            yl = jnp.where(lane < 8, ghost_lo, pltpu.roll(c, 8, 1))
            yh = jnp.where(lane >= 120, ghost_hi, pltpu.roll(c, 120, 1))
            zl = jnp.where(z8 == 0, pltpu.roll(c, 121, 1), pltpu.roll(c, 1, 1))
            zu = jnp.where(z8 == 7, pltpu.roll(c, 7, 1), pltpu.roll(c, 127, 1))
            lap = (yl + yh) + (up + dn) + (zl + zu) - 6.0 * c
            values.append(c + kappa * lap - 0.25 * (c - zl))
            rates.append(crate[pl.ds(x, 1), :])
        for n, new in enumerate(chemistry(wc_ref[...], values, rates, F)):
            cnew[4 * group + n] = new
    new_rows = lambda x: cnew[x]
    row_send[1, 0] = new_rows(0)
    row_send[1, 1] = new_rows(size_x - 1)
    col_send[1, 0] = pack(new_rows, 0)
    col_send[1, 1] = pack(new_rows, size_x - 1)
    new_halos = halos(1)

    parents = [jnp.full((F, 128), refine_ref[p], jnp.int32) for p in range(4)]

    def rings(level, rows_of):
        mid = size_x // 2
        row_at = (hx[level, 0], rows_of(mid - 1), rows_of(mid), hx[level, 1])
        col_at = (hy[level, 0], cols[level, 0], cols[level, 1], hy[level, 1])

        def joined(lo, hi, half):
            if half == 0:
                return jnp.where(first_half, lo, pltpu.roll(hi, 64, 1))
            return jnp.where(first_half, pltpu.roll(lo, 64, 1), hi)

        all_rings = []
        for p in range(4):
            a, b = p // 2, p % 2
            all_rings.append(
                (joined(row_at[a], row_at[a + 2], b), joined(col_at[b], col_at[b + 2], a))
            )
        for k in range(4):
            for side in range(2):
                value = jnp.zeros((F, 128), F32)
                for p in range(4):
                    value = jnp.where(parents[p] == k, all_rings[p][side], value)
                if k < 2:
                    ring_local[level, k, side] = value
                else:
                    ring_send[level, k - 2, side] = value
        return send(8 + level, ring_send.at[level], ring_recv.at[level], (right, gy))

    ring_old = rings(0, old_rows)
    cols[1, 0] = pack(new_rows, size_x // 2 - 1)
    cols[1, 1] = pack(new_rows, size_x // 2)

    stores = []

    def store(s):
        for h in range(2):
            copy = pltpu.make_async_copy(
                fout.at[s, h], fine_out_hbm.at[s, :, pl.ds(h * 128, 128)], out_sem.at[2 * s + h]
            )
            copy.start()
            stores.append(copy)

    half = size_x // 4

    def send_means(s):
        for j in range(half):
            mean_send[s - 2, j] = jnp.where(first_half, means[s, j], means[s, j + half])
        return send(8 + s, mean_send.at[s - 2], mean_recv.at[s - 2], (left, gy))

    for s in (2, 3):
        fine_step(s, 0)
    correct(0)
    correct(1)
    for copy in new_halos:
        copy.wait_recv()
    ring_new = rings(1, new_rows)
    fine_step(0, 1)
    store(0)
    ring_old.wait_recv()
    correct(2)
    correct(3)
    ring_new.wait_recv()
    fine_step(2, 1)
    sent_2 = send_means(2)
    store(2)
    fine_step(3, 1)
    sent_3 = send_means(3)
    store(3)
    fine_step(1, 1)
    store(1)
    sent_2.wait_recv()
    sent_3.wait_recv()

    for x in range(size_x):
        a, X = x // (size_x // 2), x % (size_x // 2)
        full = [means[0, X], means[1, X]]
        for k in range(2):
            packed = mean_recv[k, X % half]
            turned = pltpu.roll(packed, 64, 1)
            low, high = (packed, turned) if X < half else (turned, packed)
            full.append(jnp.where(first_half, low, high))
        owner = jnp.where(first_half, parents[2 * a], parents[2 * a + 1])
        value = new_rows(x)
        for k in range(4):
            value = jnp.where(owner == k, full[k], value)
        cout[pl.ds(x, F, stride=size_x), :] = value
    last = pltpu.make_async_copy(cout, coarse_out_hbm, out_sem.at[8])
    last.start()
    stores.append(last)
    for copy in old_halos + new_halos + [ring_old, ring_new, sent_2, sent_3]:
        copy.wait_send()
    for copy in stores:
        copy.wait()


def body(coarse_state, coarse_rate, fine_state, fine_rate, refine_to, parent_of, kappa, reaction):
    fields, size_x, merged = coarse_state.shape
    slots = fine_state.shape[0]
    fine_merged = fine_state.shape[3]
    flat = fields * size_x
    any_spec = pl.BlockSpec(memory_space=pl.ANY)
    smem = pl.BlockSpec(memory_space=pltpu.SMEM)
    vmem = pl.BlockSpec(memory_space=pltpu.VMEM)
    V = pltpu.VMEM
    tile = (fields, 128)
    coarse_out, fine_out = pl.pallas_call(
        functools.partial(
            kernel, lax.axis_size("gx"), lax.axis_size("gy"), fields, size_x, slots
        ),
        out_shape=(
            jax.ShapeDtypeStruct((flat, merged), F32),
            jax.ShapeDtypeStruct((slots, flat, fine_merged), F32),
        ),
        in_specs=[smem, smem, any_spec, any_spec, any_spec, any_spec, vmem, vmem],
        out_specs=(any_spec, any_spec),
        scratch_shapes=[
            V((flat, 128), F32),
            V((size_x, 128), F32),
            V((slots, 2, flat, 128), F32),
            V((slots, size_x, fine_merged), F32),
            V((slots, 2, flat, 128), F32),
            V((flat, 128), F32),
            V((slots, size_x + 2, fields, fine_merged), F32),
            V((slots, size_x + 2, fields, fine_merged), F32),
            V((2, 2) + tile, F32),
            V((2, 2) + tile, F32),
            V((2, 2) + tile, F32),
            V((2, 2) + tile, F32),
            V((size_x,) + tile, F32),
            V((2, 2) + tile, F32),
            V((2, 2, 2) + tile, F32),
            V((2, 2, 2) + tile, F32),
            V((2, 2, 2) + tile, F32),
            V((slots, size_x // 2) + tile, F32),
            V((2, size_x // 4) + tile, F32),
            V((2, size_x // 4) + tile, F32),
            V((4 * fields, 3 * fields), BF16),
            V((4 * fields, 3 * fields), BF16),
            V((slots, size_x, 8, fine_merged), F32),
            V((slots, size_x // 4, 8, 128), F32),
            pltpu.SemaphoreType.DMA((11,)),
            pltpu.SemaphoreType.DMA((9,)),
            pltpu.SemaphoreType.DMA((12,)),
            pltpu.SemaphoreType.DMA((12,)),
        ],
        compiler_params=pltpu.CompilerParams(
            collective_id=0, has_side_effects=True, vmem_limit_bytes=67043328
        ),
    )(
        refine_to, parent_of, coarse_state.reshape(flat, merged), coarse_rate,
        fine_state.reshape(slots, flat, fine_merged), fine_rate, kappa.reshape(1, fields), reaction,
    )
    return coarse_out.reshape(coarse_state.shape), fine_out.reshape(fine_state.shape)


def solution(mesh):
    in_specs = (
        P(None, "gx", "gy"),
        P("gx", "gy"),
        P(("gx", "gy"), None, None, None),
        P(("gx", "gy"), None, None),
        P(("gx", "gy")),
        P(("gx", "gy")),
        P(),
        P(),
    )
    out_specs = (P(None, "gx", "gy"), P(("gx", "gy"), None, None, None))
    return jax.shard_map(body, mesh=mesh, in_specs=in_specs, out_specs=out_specs, check_vma=False)
```

profile of v0, /device:TPU:0, one launch (start us, length us, event | category | flops | bytes accessed | tf_op | source)
XLA Modules:
  0.0 33.5 jit_solution(2274975733874195334)
XLA Ops:
  0.6 28.6 %shard_map.95 = (f32[384,128]{1,0:T(8,128)}, f32[4,384,256]{2,1,0:T(8,128)}) custom-call(s32[4]{0:T(128)} %refine_ref.1, s32[4]{0:T(128)} %parent_ref.1, f32[384,128]{1,0:T(8,128)} %bitcast.8, f32[16,128]{1,0:T(8,128)} %crate_hbm.1, f32[4,384,256]{2,1,0:T(8,128)} %bitcast.6, f32[4,16,256]{2,1,0:T(8,128)} %frate_hbm.1, f32[1,24]{1,0:T(1,128)} %bitcast.9, ...), custom_call_target="tpu_custom_call" | custom-call | tf_op jit(solution)/shard_map/pallas_call | solution.py:407
  29.3 1.6 %copy.12 = f32[24,16,128]{2,1,0:T(8,128)} copy(f32[24,16,128]{2,1,0:T(8,128)} %bitcast.7) | data formatting | bytes 393216
  30.9 2.7 %copy.13 = f32[4,24,16,256]{3,2,1,0:T(8,128)} copy(f32[4,24,16,256]{3,2,1,0:T(8,128)} %bitcast.5) | data formatting | bytes 3145728
where the time goes:
time: 33.8 us; the launch traced here: 33.5 us
  Pallas kernels  28.6 us (85%)
  local copies, waits for them, and re-layouts  4.28 us (13%)
  between operations  0.64 us (2%)
    pallas_call x1, Pallas kernels, body(): pl.pallas_call(functools.partial(kernel, lax.axis_size('gx'), lax.axis_si...  28.6 us
    unnamed x2, local copies, waits for them, and re-layouts  4.28 us

commit v1 on v0

--- a/solution.py
+++ b/solution.py
@@ -59,12 +59,12 @@
 
 def kernel(
     n_gx, n_gy, fields, size_x, slots,
-    refine_ref, parent_ref, coarse_hbm, crate_hbm, fine_hbm, frate_hbm, kappa_ref, reaction_ref,
-    coarse_out_hbm, fine_out_hbm,
-    cin, crate, fin, frate, fout, cout,
+    refine_hbm, parent_hbm, coarse_hbm, crate_hbm, fine_hbm, frate_hbm, kappa_hbm, reaction_hbm,
+    cout, fout,
+    refine_ref, parent_ref, kappa_ref, reaction_ref, cin, crate, fin, frate,
     buf_a, buf_b, row_send, col_send, hx, hy, cnew, cols, ring_local, ring_send, ring_recv,
     means, mean_send, mean_recv, wf_ref, wc_ref, rate8, edge_rate,
-    in_sem, out_sem, send_sem, recv_sem,
+    in_sem, send_sem, recv_sem,
 ):
     F = fields
     fine_cols = frate.shape[2]
@@ -74,6 +74,10 @@
     left = lax.rem(gx + n_gx - 1, n_gx)
     above = lax.rem(gy + 1, n_gy)
     below = lax.rem(gy + n_gy - 1, n_gy)
+
+    barrier = pltpu.get_barrier_semaphore()
+    for target in ((left, gy), (right, gy), (gx, below), (gx, above)):
+        pl.semaphore_signal(barrier, inc=1, device_id=target, device_id_type=MESH)
 
     loads = [
         pltpu.make_async_copy(coarse_hbm, cin, in_sem.at[0]),
@@ -88,12 +92,14 @@
                     fine_hbm.at[s, :, pl.ds(h * 128, 128)], fin.at[s, h], in_sem.at[3 + 2 * s + h]
                 )
             )
-    for copy in loads + fine_loads:
+    small = [
+        pltpu.make_async_copy(reaction_hbm, reaction_ref, in_sem.at[11]),
+        pltpu.make_async_copy(kappa_hbm, kappa_ref, in_sem.at[12]),
+        pltpu.make_async_copy(refine_hbm, refine_ref, in_sem.at[13]),
+        pltpu.make_async_copy(parent_hbm, parent_ref, in_sem.at[14]),
+    ]
+    for copy in loads[:1] + small + fine_loads + loads[1:]:
         copy.start()
-
-    barrier = pltpu.get_barrier_semaphore()
-    for target in ((left, gy), (right, gy), (gx, below), (gx, above)):
-        pl.semaphore_signal(barrier, inc=1, device_id=target, device_id_type=MESH)
 
     def send(n, src, dst, target):
         copy = pltpu.make_async_remote_copy(
@@ -133,6 +139,8 @@
 
     cols[0, 0] = pack(old_rows, size_x // 2 - 1)
     cols[0, 1] = pack(old_rows, size_x // 2)
+    for copy in small:
+        copy.wait()
     power_list, high_part = powers(reaction_ref[...], F)
     wf_ref[...] = chem_weights(power_list, high_part, 0.125)
     wc_ref[...] = chem_weights(power_list, high_part, 0.25)
@@ -331,16 +339,6 @@
     cols[1, 0] = pack(new_rows, size_x // 2 - 1)
     cols[1, 1] = pack(new_rows, size_x // 2)
 
-    stores = []
-
-    def store(s):
-        for h in range(2):
-            copy = pltpu.make_async_copy(
-                fout.at[s, h], fine_out_hbm.at[s, :, pl.ds(h * 128, 128)], out_sem.at[2 * s + h]
-            )
-            copy.start()
-            stores.append(copy)
-
     half = size_x // 4
 
     def send_means(s):
@@ -356,19 +354,15 @@
         copy.wait_recv()
     ring_new = rings(1, new_rows)
     fine_step(0, 1)
-    store(0)
     ring_old.wait_recv()
     correct(2)
     correct(3)
     ring_new.wait_recv()
     fine_step(2, 1)
     sent_2 = send_means(2)
-    store(2)
     fine_step(3, 1)
     sent_3 = send_means(3)
-    store(3)
     fine_step(1, 1)
-    store(1)
     sent_2.wait_recv()
     sent_3.wait_recv()
 
@@ -385,12 +379,24 @@
         for k in range(4):
             value = jnp.where(owner == k, full[k], value)
         cout[pl.ds(x, F, stride=size_x), :] = value
-    last = pltpu.make_async_copy(cout, coarse_out_hbm, out_sem.at[8])
-    last.start()
-    stores.append(last)
     for copy in old_halos + new_halos + [ring_old, ring_new, sent_2, sent_3]:
         copy.wait_send()
-    for copy in stores:
+
+
+def store_kernel(cout, fout, coarse_out_hbm, fine_out_hbm, sem):
+    copies = [pltpu.make_async_copy(cout, coarse_out_hbm, sem.at[0])]
+    slots = fout.shape[0]
+    for s in range(slots):
+        for h in range(2):
+            copies.append(
+                pltpu.make_async_copy(
+                    fout.at[s, h], fine_out_hbm.at[s, :, pl.ds(h * 128, 128)],
+                    sem.at[1 + 2 * s + h],
+                )
+            )
+    for copy in copies:
+        copy.start()
+    for copy in copies:
         copy.wait()
 
 
@@ -400,27 +406,25 @@
     fine_merged = fine_state.shape[3]
     flat = fields * size_x
     any_spec = pl.BlockSpec(memory_space=pl.ANY)
-    smem = pl.BlockSpec(memory_space=pltpu.SMEM)
     vmem = pl.BlockSpec(memory_space=pltpu.VMEM)
     V = pltpu.VMEM
     tile = (fields, 128)
-    coarse_out, fine_out = pl.pallas_call(
+    cout, fout = pl.pallas_call(
         functools.partial(
             kernel, lax.axis_size("gx"), lax.axis_size("gy"), fields, size_x, slots
         ),
-        out_shape=(
-            jax.ShapeDtypeStruct((flat, merged), F32),
-            jax.ShapeDtypeStruct((slots, flat, fine_merged), F32),
-        ),
-        in_specs=[smem, smem, any_spec, any_spec, any_spec, any_spec, vmem, vmem],
-        out_specs=(any_spec, any_spec),
+        out_shape=(V((flat, 128), F32), V((slots, 2, flat, 128), F32)),
+        in_specs=[any_spec] * 8,
+        out_specs=(vmem, vmem),
         scratch_shapes=[
+            pltpu.SMEM((slots,), jnp.int32),
+            pltpu.SMEM((slots,), jnp.int32),
+            V((1, fields), F32),
+            V((fields, fields), F32),
             V((flat, 128), F32),
             V((size_x, 128), F32),
             V((slots, 2, flat, 128), F32),
             V((slots, size_x, fine_merged), F32),
-            V((slots, 2, flat, 128), F32),
-            V((flat, 128), F32),
             V((slots, size_x + 2, fields, fine_merged), F32),
             V((slots, size_x + 2, fields, fine_merged), F32),
             V((2, 2) + tile, F32),
@@ -439,18 +443,34 @@
             V((4 * fields, 3 * fields), BF16),
             V((slots, size_x, 8, fine_merged), F32),
             V((slots, size_x // 4, 8, 128), F32),
-            pltpu.SemaphoreType.DMA((11,)),
-            pltpu.SemaphoreType.DMA((9,)),
+            pltpu.SemaphoreType.DMA((15,)),
             pltpu.SemaphoreType.DMA((12,)),
             pltpu.SemaphoreType.DMA((12,)),
         ],
         compiler_params=pltpu.CompilerParams(
-            collective_id=0, has_side_effects=True, vmem_limit_bytes=67043328
+            collective_id=0, has_side_effects=True, vmem_limit_bytes=24 * 2**20
         ),
     )(
-        refine_to, parent_of, coarse_state.reshape(flat, merged), coarse_rate,
-        fine_state.reshape(slots, flat, fine_merged), fine_rate, kappa.reshape(1, fields), reaction,
+        *[
+            pltpu.with_memory_space_constraint(array, pltpu.HBM)
+            for array in (
+                refine_to, parent_of, coarse_state.reshape(flat, merged), coarse_rate,
+                fine_state.reshape(slots, flat, fine_merged), fine_rate,
+                kappa.reshape(1, fields), reaction,
+            )
+        ]
     )
+    coarse_out, fine_out = pl.pallas_call(
+        store_kernel,
+        out_shape=(
+            jax.ShapeDtypeStruct((flat, merged), F32),
+            jax.ShapeDtypeStruct((slots, flat, fine_merged), F32),
+        ),
+        in_specs=[vmem, vmem],
+        out_specs=(any_spec, any_spec),
+        scratch_shapes=[pltpu.SemaphoreType.DMA((1 + 2 * slots,))],
+        compiler_params=pltpu.CompilerParams(vmem_limit_bytes=8 * 2**20),
+    )(cout, fout)
     return coarse_out.reshape(coarse_state.shape), fine_out.reshape(fine_state.shape)
 
 

time: 33.8 us -> 29.5 us (0.87)
  local copies, waits for them, and re-layouts: 4.28 us -> 0 us
    unnamed x2 -> x0, local copies, waits for them, and re-layouts: 4.28 us -> none
    pallas_call x0 -> x1, Pallas kernels: none -> 1.27 us  [body(): pl.pallas_call(store_kernel, out_shape=(jax.ShapeDtypeStruct((flat, merge...]
    pallas_call x1, Pallas kernels: 28.6 us -> 27.4 us  [body(): pl.pallas_call(functools.partial(kernel, lax.axis_size('gx'), lax.axis_si...]
where the time goes in v1:
time: 29.5 us; the launch traced here: 29.4 us
  Pallas kernels  28.7 us (97%)
  between operations  0.64 us (2%)
    pallas_call x1, Pallas kernels, body(): pl.pallas_call(functools.partial(kernel, lax.axis_size('gx'), lax.axis_si...  27.4 us
    pallas_call x1, Pallas kernels, body(): pl.pallas_call(store_kernel, out_shape=(jax.ShapeDtypeStruct((flat, merge...  1.27 us

profile of v1, /device:TPU:0, one launch (start us, length us, event | category | flops | bytes accessed | tf_op | source)
XLA Modules:
  0.0 29.4 jit_solution(3447910766575192015)
XLA Ops:
  0.6 27.4 %shard_map.95 = (f32[384,128]{1,0:T(8,128)S(1)}, f32[4,2,384,128]{3,2,1,0:T(8,128)S(1)}) custom-call(s32[4]{0:T(128)} %refine_hbm.1, s32[4]{0:T(128)} %parent_hbm.1, f32[384,128]{1,0:T(8,128)} %bitcast.6, f32[16,128]{1,0:T(8,128)} %crate_hbm.1, f32[4,384,256]{2,1,0:T(8,128)} %bitcast.5, f32[4,16,256]{2,1,0:T(8,128)} %frate_hbm.1, f32[1,24]{1,0:T(1,128)} %bitcast.7, ...), custom_call_target="tpu_custom_call" | custom-call | tf_op jit(solution)/shard_map/pallas_call | solution.py:412
  28.1 1.3 %shard_map.96 = (f32[384,128]{1,0:T(8,128)}, f32[4,384,256]{2,1,0:T(8,128)}) custom-call(f32[384,128]{1,0:T(8,128)S(1)} %get-tuple-element.6.cout, f32[4,2,384,128]{3,2,1,0:T(8,128)S(1)} %get-tuple-element.7.fout), custom_call_target="tpu_custom_call" | custom-call | tf_op jit(solution)/shard_map/pallas_call | solution.py:463

commit v2 on v1

v2 whole, which is shorter than its diff:
```python
import functools
import jax
import jax.numpy as jnp
from jax import lax
from jax.experimental import pallas as pl
from jax.experimental.pallas import tpu as pltpu
from jax.sharding import PartitionSpec as P

MESH = pl.DeviceIdType.MESH
F32 = jnp.float32
BF16 = jnp.bfloat16


def lanes(rows):
    return lax.broadcasted_iota(jnp.int32, (rows, 128), 1)


def pick(table, index):
    return jnp.take_along_axis(table, index, axis=1)


def powers(reaction, fields):
    row = lax.broadcasted_iota(jnp.int32, (fields, 3 * fields), 0)
    col = lax.broadcasted_iota(jnp.int32, (fields, 3 * fields), 1)
    power = (col % fields == row).astype(F32)
    result = []
    for _ in range(4):
        power = jnp.dot(
            reaction, power, precision=lax.Precision.HIGHEST, preferred_element_type=F32
        )
        result.append(power)
    return result, col < 2 * fields


def chem_weights(power_list, high_part, step):
    parts = []
    for count, (choose, power) in enumerate(zip((4.0, 6.0, 4.0, 1.0), power_list)):
        value = power * (choose * step ** (count + 1))
        high = value.astype(BF16).astype(F32)
        parts.append(jnp.where(high_part, high, value - high))
    return jnp.concatenate(parts, axis=0).astype(BF16)


def chemistry(weights, values, rates, fields):
    wide = jnp.concatenate(values, axis=1)
    high = wide.astype(BF16).astype(F32)
    low = wide - high
    stacked = jnp.concatenate([high, low, high], axis=0).astype(BF16)
    product = jnp.dot(weights, stacked, preferred_element_type=F32)
    out = []
    for n, (value, rate) in enumerate(zip(values, rates)):
        part = [
            product[q * fields : (q + 1) * fields, n * 128 : (n + 1) * 128] for q in range(4)
        ]
        rate = jnp.broadcast_to(rate, value.shape)
        out.append(value + rate * (part[0] + rate * (part[1] + rate * (part[2] + rate * part[3]))))
    return out


def shift_matrix(group):
    row = lax.broadcasted_iota(jnp.int32, (256, 128), 0) % 128
    col = lax.broadcasted_iota(jnp.int32, (256, 128), 1)
    same = row // group == col // group
    lower = same & ((col - row + group) % group == 1)
    upper = same & ((row - col + group) % group == 1)
    side = (row - col == group) | (col - row == group)
    around = jnp.where(lower | upper | side, 1.0, 0.0)
    return jnp.concatenate([around, jnp.where(lower, 0.25, 0.0)], axis=1).astype(BF16)


def shifted_sums(matrix, rows):
    high = rows.astype(BF16)
    low = (rows - high.astype(F32)).astype(BF16)
    return jnp.dot(
        jnp.concatenate([high, low], axis=1), matrix, preferred_element_type=F32
    )


def turn(value, shift):
    shift = shift % 128
    return pltpu.roll(value, shift, 1) if shift else value


def kernel(
    n_gx, n_gy, fields, size_x, slots,
    refine_hbm, parent_hbm, coarse_hbm, crate_hbm, fine_hbm, frate_hbm, kappa_hbm, reaction_hbm,
    cout, fout,
    refine_ref, parent_ref, kappa_ref, reaction_ref, cin, crate, fin, frate, buf_b,
    row_send, col_send, corner_send, rx, ry, rd, cnew, cols, rate_cols,
    ring, ring_send, ring_recv, means, mean_send, mean_recv,
    cols_new, wf_ref, wc_ref, rate8, edge_rate, shift_f, shift_c,
    in_sem, send_sem, recv_sem,
):
    F = fields
    fine_cols = frate.shape[2]
    last = size_x - 1
    mid = size_x // 2
    gx = lax.axis_index("gx")
    gy = lax.axis_index("gy")
    right = lax.rem(gx + 1, n_gx)
    left = lax.rem(gx + n_gx - 1, n_gx)
    above = lax.rem(gy + 1, n_gy)
    below = lax.rem(gy + n_gy - 1, n_gy)

    barrier = pltpu.get_barrier_semaphore()
    for target in (
        (right, gy), (left, gy), (gx, above), (gx, below),
        (right, above), (right, below), (left, above), (left, below),
    ):
        pl.semaphore_signal(barrier, inc=1, device_id=target, device_id_type=MESH)

    load_coarse = pltpu.make_async_copy(coarse_hbm, cin, in_sem.at[0])
    load_crate = pltpu.make_async_copy(crate_hbm, crate, in_sem.at[1])
    load_frate = pltpu.make_async_copy(frate_hbm, frate, in_sem.at[2])
    fine_loads = [
        [
            pltpu.make_async_copy(
                fine_hbm.at[s, :, pl.ds(h * 128, 128)], fin.at[s, h], in_sem.at[3 + 2 * s + h]
            )
            for h in range(2)
        ]
        for s in range(slots)
    ]
    small = [
        pltpu.make_async_copy(reaction_hbm, reaction_ref, in_sem.at[11]),
        pltpu.make_async_copy(kappa_hbm, kappa_ref, in_sem.at[12]),
        pltpu.make_async_copy(refine_hbm, refine_ref, in_sem.at[13]),
        pltpu.make_async_copy(parent_hbm, parent_ref, in_sem.at[14]),
    ]
    order = (2, 3, 0, 1)
    for copy in [load_coarse, load_crate] + small + [load_frate]:
        copy.start()
    for s in order:
        for copy in fine_loads[s]:
            copy.start()

    def send(n, src, dst, target):
        copy = pltpu.make_async_remote_copy(
            src_ref=src, dst_ref=dst, send_sem=send_sem.at[n], recv_sem=recv_sem.at[n],
            device_id=target, device_id_type=MESH,
        )
        copy.start()
        return copy

    lane = lanes(F)
    lane8 = lanes(8)
    first_half = lane < 64

    shift_f[...] = shift_matrix(16)
    shift_c[...] = shift_matrix(8)

    def pack(rows_of, y, at):
        total = None
        for x in range(size_x):
            moved = turn(rows_of(x), (x - y) * 8)
            total = moved if total is None else jnp.where(at // 8 == x, moved, total)
        return total

    near, far, rate_rows = pl.ds(0, F), pl.ds(F, F), pl.ds(2 * F, 8)
    old_row = lambda x: cin[pl.ds(x, F, stride=size_x), :]
    crate_row = lambda x: jnp.broadcast_to(crate[pl.ds(x, 1), :], (8, 128))

    load_coarse.wait()
    load_crate.wait()
    for side, (x0, x1) in enumerate(((0, 1), (last, last - 1))):
        row, rate = old_row(x0), crate_row(x0)
        row_send[side, near] = row
        row_send[side, far] = old_row(x1)
        row_send[side, rate_rows] = rate
        pieces = [row[8 * j : 8 * j + 8] for j in range(F // 8)] + [rate]
        corner = pieces[0]
        for j, piece in enumerate(pieces):
            if j:
                corner = jnp.where(lane8 // 8 == j, turn(piece, 8 * j), corner)
            corner = jnp.where(lane8 // 8 == 8 + j, turn(piece, 8 * j - 56), corner)
        corner_send[side] = corner
    for side, (y0, y1) in enumerate(((0, 1), (last, last - 1))):
        col_send[side, near] = pack(old_row, y0, lane)
        col_send[side, far] = pack(old_row, y1, lane)
        col_send[side, rate_rows] = pack(crate_row, y0, lane8)

    for copy in small:
        copy.wait()
    power_list, high_part = powers(reaction_ref[...], F)
    wf_ref[...] = chem_weights(power_list, high_part, 0.125)
    wc_ref[...] = chem_weights(power_list, high_part, 0.25)
    diag = lax.broadcasted_iota(jnp.int32, (F, F), 0) == lax.broadcasted_iota(jnp.int32, (F, F), 1)
    kappa_col = jnp.sum(
        jnp.where(diag, jnp.broadcast_to(kappa_ref[...], (F, F)), 0.0), axis=1, keepdims=True
    )
    kappa = jnp.broadcast_to(kappa_col, (F, 128))
    kappa2 = 2.0 * kappa
    keep_fine = 0.75 - 6.0 * kappa2
    keep_coarse = 0.75 - 6.0 * kappa

    pl.semaphore_wait(barrier, 8)
    to_right = [
        send(0, row_send.at[1], rx.at[0], (right, gy)),
        send(4, corner_send.at[1], rd.at[0], (right, above)),
        send(5, corner_send.at[1], rd.at[1], (right, below)),
    ]
    to_side = [
        send(2, col_send.at[1], ry.at[0], (gx, above)),
        send(3, col_send.at[0], ry.at[1], (gx, below)),
    ]
    to_left = [
        send(1, row_send.at[0], rx.at[1], (left, gy)),
        send(6, corner_send.at[0], rd.at[2], (left, above)),
        send(7, corner_send.at[0], rd.at[3], (left, below)),
    ]
    for n in range(4):
        cols[n] = pack(old_row, mid - 2 + n, lane)
    for n in range(2):
        rate_cols[n] = pack(crate_row, mid - 1 + n, lane8)

    def wide(rate):
        return jnp.concatenate([rate] * (F // 8), axis=0)

    def from_corner(m, src, dst):
        tile = rd[m]
        return jnp.concatenate([turn(tile, dst - src - 8 * j) for j in range(F // 8)], axis=0)

    def coarse_tiles(tiles):
        centers = jnp.concatenate([tile[0] for tile in tiles], axis=0)
        shifted = shifted_sums(shift_c[...], centers)
        values = []
        for n, (center, lo, hi, ghost_lo, ghost_hi, _) in enumerate(tiles):
            part = shifted[F * n : F * n + F]
            edge = 0.0 if ghost_hi is None else jnp.where(lane >= 120, ghost_hi, 0.0)
            edge = jnp.where(lane < 8, ghost_lo, edge)
            lateral = (lo + hi) + (part[:, :128] + edge)
            values.append(keep_coarse * center + kappa * lateral + part[:, 128:])
        return values

    def react(values, rates):
        out = []
        for at in range(0, len(values), 4):
            out += chemistry(wc_ref[...], values[at : at + 4], rates[at : at + 4], F)
        return out

    def row_tile(x):
        if x == -1:
            return (
                rx[0, near], rx[0, far], old_row(0),
                from_corner(0, 64, 0), from_corner(1, 0, 120), wide(rx[0, rate_rows]),
            )
        if x == size_x:
            return (
                rx[1, near], old_row(last), rx[1, far],
                from_corner(2, 64, 0), from_corner(3, 0, 120), wide(rx[1, rate_rows]),
            )
        return (
            old_row(x),
            old_row(x - 1) if x else rx[0, near],
            old_row(x + 1) if x < last else rx[1, near],
            turn(ry[0, near], -8 * x), turn(ry[1, near], 120 - 8 * x),
            crate[pl.ds(x, 1), :],
        )

    def joined(lo, hi, half):
        if half == 0:
            return jnp.where(first_half, lo, turn(hi, 64))
        return jnp.where(first_half, turn(lo, 64), hi)

    parents = [jnp.full((F, 128), refine_ref[p], jnp.int32) for p in range(4)]

    def ring_tiles(row_at, col_at):
        return [
            (
                joined(row_at[p // 2], row_at[p // 2 + 2], p % 2),
                joined(col_at[p % 2], col_at[p % 2 + 2], p // 2),
            )
            for p in range(4)
        ]

    def chosen(tiles, k, side):
        value = jnp.zeros((F, 128), F32)
        for p in range(4):
            value = jnp.where(parents[p] == k, tiles[p][side], value)
        return value

    def send_ring(level, row_at, col_at):
        tiles = ring_tiles(row_at, col_at)
        for k in range(2):
            for side in range(2):
                ring_send[level, k, side] = chosen(tiles, k + 2, side)
        return send(8 + level, ring_send.at[level], ring_recv.at[level], (right, gy))

    corner_lanes = (lane // 8 == 7) | (lane // 8 == 15)

    def end_share(share):
        return (
            jnp.where(corner_lanes, turn(share, 56), 0.0), jnp.where(corner_lanes, share, 0.0)
        )

    for copy in to_right + to_side:
        copy.wait_recv()
    old_cols = [ry[0, near], cols[1], cols[2], ry[1, near]]
    ring_old = send_ring(
        0, [rx[0, near], old_row(mid - 1), old_row(mid), old_row(mid)], old_cols
    )
    tiles = [
        row_tile(-1), row_tile(mid - 1), row_tile(mid), row_tile(0),
        (ry[0, near], ry[0, far], col_send[0, near], from_corner(0, 64, 0), None,
         wide(ry[0, rate_rows])),
        (cols[1], cols[0], cols[2], turn(rx[0, near], -8 * (mid - 1)), None, wide(rate_cols[0])),
        (cols[2], cols[1], cols[3], turn(rx[0, near], -8 * mid), None, wide(rate_cols[1])),
        (ry[1, near], col_send[1, near], ry[1, far], from_corner(1, 0, 0), None,
         wide(ry[1, rate_rows])),
    ]
    values = coarse_tiles(tiles)
    end = jnp.where(lane >= 120, turn(ry[1, near], 120), old_row(0))
    values.append(kappa * jnp.where(lane < 8, ry[0, near], end))
    end_rate = jnp.where(lane8 >= 120, turn(rd[1], 96), rx[0, rate_rows])
    end_rate = jnp.where(lane8 < 8, turn(rd[0], 40), end_rate)
    result = react(values, [tile[5] for tile in tiles] + [wide(end_rate)])
    new_before, new_cols = result[0], result[4:8]
    cnew[mid - 1], cnew[mid], cnew[0] = result[1:4]
    ring_new = send_ring(1, [new_before, result[1], result[2], result[2]], new_cols)
    far_share = result[8]
    for n, value in enumerate([new_before] + new_cols):
        cols_new[n] = value
    cols_new[5] = far_share

    z16 = lane % 16
    row_index = (lane // 32) * 8 + z16 // 2
    col_index = jnp.where(lane < 64, 0, 64) + z16 // 2
    target = lane % 64
    mean_index = ((target // 8) % 4) * 32 + 2 * (target % 8)
    mean_low = target // 32 == 0
    edge_lane = (lane < 16) | (lane >= 112)

    load_frate.wait()

    def spread_rate(s):
        for x in range(size_x):
            rate8[s, x] = jnp.broadcast_to(frate[s, pl.ds(x, 1), :], rate8.shape[2:])

    def fine_step(s, step, edges, done=None):
        def row_of(x, h):
            if 0 <= x < size_x:
                if step == 0:
                    return fin[s, h, pl.ds(x, F, stride=size_x), :]
                return buf_b[s, x, :, pl.ds(h * 128, 128)]
            if edges is None:
                return jnp.zeros((F, 128), F32)
            return pick(edges[0], row_index + 32 * h + (64 if x > 0 else 0))

        weights = wf_ref[...]
        live = jnp.full((F, 128), parent_ref[s], jnp.int32) >= 0
        size = size_x // 2
        for i in range(2):
            rows = [[row_of(x, h) for h in range(2)] for x in range(size * i - 1, size * i + size + 1)]
            shifted = shifted_sums(
                shift_f[...], jnp.concatenate([v for row in rows[1:-1] for v in row], axis=0)
            )
            for m in range(size // 2):
                j = size // 2 * i + m
                if edges is None:
                    ghost = 0.0
                else:
                    ghost = jnp.where(edge_lane, pick(edges[1], col_index + 8 * j), 0.0)
                values, rates = [], []
                for n in range(2):
                    r = 2 * m + n + 1
                    v0, v1 = rows[r]
                    cross = [
                        jnp.where(lane >= 112, turn(v1, 112), ghost),
                        jnp.where(lane < 16, turn(v0, 16), ghost),
                    ]
                    for h in range(2):
                        at = F * (2 * (r - 1) + h)
                        part = shifted[at : at + F]
                        lateral = (part[:, :128] + cross[h]) + (rows[r - 1][h] + rows[r + 1][h])
                        values.append(keep_fine * rows[r][h] + kappa2 * lateral + part[:, 128:])
                        rates.append(wide(rate8[s, 2 * j + n, :, pl.ds(h * 128, 128)]))
                new = chemistry(weights, values, rates, F)
                if step == 0:
                    for n in range(2):
                        for h in range(2):
                            buf_b[s, 2 * j + n, :, pl.ds(h * 128, 128)] = new[2 * n + h]
                else:
                    new = [jnp.where(live, v, 0.0) for v in new]
                    for n in range(2):
                        for h in range(2):
                            fout[s, h, pl.ds(2 * j + n, F, stride=size_x), :] = new[2 * n + h]
                    picked = []
                    for h in range(2):
                        total = new[h] + new[2 + h]
                        total = total + turn(total, 127)
                        total = total + turn(total, 112)
                        picked.append(pick(total, mean_index))
                    means[s, j] = 0.125 * jnp.where(mean_low, picked[0], picked[1])
            if done is not None:
                done(i)

    def pack_edge_rate(s):
        for q in range(size_x // 4):
            total = jnp.zeros((8, 128), F32)
            for n in range(4):
                lo = turn(rate8[s, 4 * q + n, :, pl.ds(0, 128)], 16 * n)
                hi = turn(rate8[s, 4 * q + n, :, pl.ds(fine_cols - 128, 128)], 16 * n - 48)
                total = jnp.where(lane8 // 16 == n, lo, total)
                total = jnp.where(lane8 // 16 == 4 + n, hi, total)
            edge_rate[s - 2, q] = total

    edge_index = (lane // 64) * 64 + ((lane % 64) // 32) * 8 + z16 // 2

    def correct(s):
        edge_x, edge_y = ring[0, s, 0], ring[0, s, 1]
        values, rates = [], []
        for side, x in ((0, 0), (1, last)):
            for h in range(2):
                values.append(kappa2 * pick(edge_x, row_index + 64 * side + 32 * h))
                rates.append(wide(rate8[s, x, :, pl.ds(h * 128, 128)]))
        for q in range(size_x // 4):
            values.append(kappa2 * pick(edge_y, edge_index + 16 * q))
            rates.append(wide(edge_rate[s - 2, q]))
        share = chemistry(wf_ref[...], values, rates, F)
        for x in range(size_x):
            q, n = x // 4, x % 4
            both = share[4 + q]
            added = [
                jnp.where(lane < 16, turn(both, -16 * n), 0.0),
                jnp.where(lane >= 112, turn(both, 48 - 16 * n), 0.0),
            ]
            for h in range(2):
                if x == 0:
                    added[h] = added[h] + share[h]
                if x == last:
                    added[h] = added[h] + share[2 + h]
                here = (s, x, slice(None), pl.ds(h * 128, 128))
                buf_b[here] = buf_b[here] + added[h]

    def mid_edges(s):
        return [0.5 * (ring[0, s, side] + ring[1, s, side]) for side in range(2)]

    for s in (2, 3):
        for copy in fine_loads[s]:
            copy.wait()
        spread_rate(s)
        pack_edge_rate(s)
        fine_step(s, 0, None)

    homes = [jnp.full((F, 128), parent_ref[s], jnp.int32) for s in range(slots)]

    def take_ring(level, row):
        turned = turn(row, 64)
        for k in range(2):
            home = homes[k + 2]
            value = ring_recv[level, k, 0]
            value = jnp.where((home == 2) & ~first_half, turned, value)
            value = jnp.where((home == 3) & ~first_half, row, value)
            ring[level, k + 2, 0] = value
            value = ring_recv[level, k, 1]
            if level:
                fix = end_share(cols_new[5])
                added = jnp.where(home == 2, fix[0], jnp.where(home == 3, fix[1], 0.0))
                value = value + added
            ring[level, k + 2, 1] = value

    ring_old.wait_recv()
    take_ring(0, old_row(0))
    for s in (2, 3):
        correct(s)
    ring_new.wait_recv()
    take_ring(1, cnew[0])

    sent = []
    for s in (2, 3):
        def send_part(i, s=s):
            size = size_x // 8
            for m in range(size):
                j = 2 * (size * i + m)
                mean_send[s - 2, i, m] = jnp.where(first_half, means[s, j], means[s, j + 1])
            sent.append(
                send(
                    10 + 2 * (s - 2) + i, mean_send.at[s - 2, i], mean_recv.at[s - 2, i], (left, gy)
                )
            )

        fine_step(s, 1, mid_edges(s), send_part)

    for copy in to_left:
        copy.wait_recv()
    rest = [x for x in range(1, size_x + 1) if x not in (mid - 1, mid)]
    values, rates = [], []
    for at in range(0, len(rest), 2):
        tiles = [row_tile(x) for x in rest[at : at + 2]]
        values += coarse_tiles(tiles)
        rates += [tile[5] for tile in tiles]
    end = jnp.where(lane < 8, from_corner(2, 64, 0), rx[1, near])
    values.append(kappa * jnp.where(lane >= 120, from_corner(3, 0, 120), end))
    end_rate = jnp.where(lane8 < 8, turn(ry[0, rate_rows], 8), crate_row(last))
    rates.append(wide(jnp.where(lane8 >= 120, ry[1, rate_rows], end_rate)))
    result = react(values, rates)
    for x, value in zip(rest[:-1], result):
        cnew[x] = value
    fix = end_share(result[-1])
    tiles_old = ring_tiles([rx[0, near], old_row(mid - 1), old_row(mid), rx[1, near]], old_cols)
    tiles_new = ring_tiles(
        [cols_new[0], cnew[mid - 1], cnew[mid], result[-2]], [cols_new[n] for n in range(1, 5)]
    )
    for p in (2, 3):
        tiles_new[p] = (tiles_new[p][0], tiles_new[p][1] + fix[p - 2])
    for k in range(2):
        for side in range(2):
            ring[0, k, side] = chosen(tiles_old, k, side)
            ring[1, k, side] = chosen(tiles_new, k, side)

    for s in (0, 1):
        for copy in fine_loads[s]:
            copy.wait()
        spread_rate(s)
        fine_step(s, 0, [ring[0, s, 0], ring[0, s, 1]])
        fine_step(s, 1, mid_edges(s))
    for copy in sent:
        copy.wait_recv()

    for x in range(size_x):
        a, X = x // mid, x % mid
        full = [means[0, X], means[1, X]]
        for k in range(2):
            packed = mean_recv[k, X // (mid // 2), (X % (mid // 2)) // 2]
            turned = turn(packed, 64)
            low, high = (packed, turned) if X % 2 == 0 else (turned, packed)
            full.append(jnp.where(first_half, low, high))
        owner = jnp.where(first_half, parents[2 * a], parents[2 * a + 1])
        value = cnew[x]
        for k in range(4):
            value = jnp.where(owner == k, full[k], value)
        cout[pl.ds(x, F, stride=size_x), :] = value
    for copy in to_right + to_side + to_left + [ring_old, ring_new] + sent:
        copy.wait_send()


def store_kernel(cout, fout, coarse_out_hbm, fine_out_hbm, sem):
    copies = [pltpu.make_async_copy(cout, coarse_out_hbm, sem.at[0])]
    slots = fout.shape[0]
    for s in range(slots):
        for h in range(2):
            copies.append(
                pltpu.make_async_copy(
                    fout.at[s, h], fine_out_hbm.at[s, :, pl.ds(h * 128, 128)],
                    sem.at[1 + 2 * s + h],
                )
            )
    for copy in copies:
        copy.start()
    for copy in copies:
        copy.wait()


def body(coarse_state, coarse_rate, fine_state, fine_rate, refine_to, parent_of, kappa, reaction):
    fields, size_x, merged = coarse_state.shape
    slots = fine_state.shape[0]
    fine_merged = fine_state.shape[3]
    flat = fields * size_x
    any_spec = pl.BlockSpec(memory_space=pl.ANY)
    vmem = pl.BlockSpec(memory_space=pltpu.VMEM)
    V = pltpu.VMEM
    tile = (fields, 128)
    cout, fout = pl.pallas_call(
        functools.partial(
            kernel, lax.axis_size("gx"), lax.axis_size("gy"), fields, size_x, slots
        ),
        out_shape=(V((flat, 128), F32), V((slots, 2, flat, 128), F32)),
        in_specs=[any_spec] * 8,
        out_specs=(vmem, vmem),
        scratch_shapes=[
            pltpu.SMEM((slots,), jnp.int32),
            pltpu.SMEM((slots,), jnp.int32),
            V((1, fields), F32),
            V((fields, fields), F32),
            V((flat, 128), F32),
            V((size_x, 128), F32),
            V((slots, 2, flat, 128), F32),
            V((slots, size_x, fine_merged), F32),
            V((slots, size_x, fields, fine_merged), F32),
            V((2, 2 * fields + 8, 128), F32),
            V((2, 2 * fields + 8, 128), F32),
            V((2, 8, 128), F32),
            V((2, 2 * fields + 8, 128), F32),
            V((2, 2 * fields + 8, 128), F32),
            V((4, 8, 128), F32),
            V((size_x,) + tile, F32),
            V((4,) + tile, F32),
            V((2, 8, 128), F32),
            V((2, slots, 2) + tile, F32),
            V((2, 2, 2) + tile, F32),
            V((2, 2, 2) + tile, F32),
            V((slots, size_x // 2) + tile, F32),
            V((2, 2, size_x // 8) + tile, F32),
            V((2, 2, size_x // 8) + tile, F32),
            V((6,) + tile, F32),
            V((4 * fields, 3 * fields), BF16),
            V((4 * fields, 3 * fields), BF16),
            V((slots, size_x, 8, fine_merged), F32),
            V((2, size_x // 4, 8, 128), F32),
            V((256, 256), BF16),
            V((256, 256), BF16),
            pltpu.SemaphoreType.DMA((15,)),
            pltpu.SemaphoreType.DMA((14,)),
            pltpu.SemaphoreType.DMA((14,)),
        ],
        compiler_params=pltpu.CompilerParams(
            collective_id=0, has_side_effects=True, vmem_limit_bytes=24 * 2**20
        ),
    )(
        *[
            pltpu.with_memory_space_constraint(array, pltpu.HBM)
            for array in (
                refine_to, parent_of, coarse_state.reshape(flat, merged), coarse_rate,
                fine_state.reshape(slots, flat, fine_merged), fine_rate,
                kappa.reshape(1, fields), reaction,
            )
        ]
    )
    coarse_out, fine_out = pl.pallas_call(
        store_kernel,
        out_shape=(
            jax.ShapeDtypeStruct((flat, merged), F32),
            jax.ShapeDtypeStruct((slots, flat, fine_merged), F32),
        ),
        in_specs=[vmem, vmem],
        out_specs=(any_spec, any_spec),
        scratch_shapes=[pltpu.SemaphoreType.DMA((1 + 2 * slots,))],
        compiler_params=pltpu.CompilerParams(vmem_limit_bytes=8 * 2**20),
    )(cout, fout)
    return coarse_out.reshape(coarse_state.shape), fine_out.reshape(fine_state.shape)


def solution(mesh):
    in_specs = (
        P(None, "gx", "gy"),
        P("gx", "gy"),
        P(("gx", "gy"), None, None, None),
        P(("gx", "gy"), None, None),
        P(("gx", "gy")),
        P(("gx", "gy")),
        P(),
        P(),
    )
    out_specs = (P(None, "gx", "gy"), P(("gx", "gy"), None, None, None))
    return jax.shard_map(body, mesh=mesh, in_specs=in_specs, out_specs=out_specs, check_vma=False)
```

time: 29.5 us -> 23.3 us (0.79)
  Pallas kernels: 28.7 us -> 22.5 us
    pallas_call x1, Pallas kernels: 27.4 us -> 21.3 us  [body(): pl.pallas_call(functools.partial(kernel, lax.axis_size('gx'), lax.axis_si...]
where the time goes in v2:
time: 23.3 us; the launch traced here: 23.2 us
  Pallas kernels  22.5 us (97%)
  between operations  0.64 us (3%)
    pallas_call x1, Pallas kernels, body(): pl.pallas_call(functools.partial(kernel, lax.axis_size('gx'), lax.axis_si...  21.3 us
    pallas_call x1, Pallas kernels, body(): pl.pallas_call(store_kernel, out_shape=(jax.ShapeDtypeStruct((flat, merge...  1.27 us

profile of v2, /device:TPU:0, one launch (start us, length us, event | category | flops | bytes accessed | tf_op | source)
XLA Modules:
  0.0 23.2 jit_solution(4313003153145873326)
XLA Ops:
  0.6 21.3 %shard_map.95 = (f32[384,128]{1,0:T(8,128)S(1)}, f32[4,2,384,128]{3,2,1,0:T(8,128)S(1)}) custom-call(s32[4]{0:T(128)} %refine_hbm.1, s32[4]{0:T(128)} %parent_hbm.1, f32[384,128]{1,0:T(8,128)} %bitcast.6, f32[16,128]{1,0:T(8,128)} %crate_hbm.1, f32[4,384,256]{2,1,0:T(8,128)} %bitcast.5, f32[4,16,256]{2,1,0:T(8,128)} %frate_hbm.1, f32[1,24]{1,0:T(1,128)} %bitcast.7, ...), custom_call_target="tpu_custom_call" | custom-call | tf_op jit(solution)/shard_map/pallas_call | solution.py:563
  21.9 1.3 %shard_map.96 = (f32[384,128]{1,0:T(8,128)}, f32[4,384,256]{2,1,0:T(8,128)}) custom-call(f32[384,128]{1,0:T(8,128)S(1)} %get-tuple-element.6.cout, f32[4,2,384,128]{3,2,1,0:T(8,128)S(1)} %get-tuple-element.7.fout), custom_call_target="tpu_custom_call" | custom-call | tf_op jit(solution)/shard_map/pallas_call | solution.py:619

commit v3 on v2

--- a/solution.py
+++ b/solution.py
@@ -41,12 +41,15 @@
     return jnp.concatenate(parts, axis=0).astype(BF16)
 
 
-def chemistry(weights, values, rates, fields):
+def chemistry_product(weights, values):
     wide = jnp.concatenate(values, axis=1)
     high = wide.astype(BF16).astype(F32)
     low = wide - high
     stacked = jnp.concatenate([high, low, high], axis=0).astype(BF16)
-    product = jnp.dot(weights, stacked, preferred_element_type=F32)
+    return jnp.dot(weights, stacked, preferred_element_type=F32)
+
+
+def chemistry_sum(product, values, rates, fields):
     out = []
     for n, (value, rate) in enumerate(zip(values, rates)):
         part = [
@@ -55,6 +58,10 @@
         rate = jnp.broadcast_to(rate, value.shape)
         out.append(value + rate * (part[0] + rate * (part[1] + rate * (part[2] + rate * part[3]))))
     return out
+
+
+def chemistry(weights, values, rates, fields):
+    return chemistry_sum(chemistry_product(weights, values), values, rates, fields)
 
 
 def shift_matrix(group):
@@ -86,10 +93,10 @@
     refine_hbm, parent_hbm, coarse_hbm, crate_hbm, fine_hbm, frate_hbm, kappa_hbm, reaction_hbm,
     cout, fout,
     refine_ref, parent_ref, kappa_ref, reaction_ref, cin, crate, fin, frate, buf_b,
-    row_send, col_send, corner_send, rx, ry, rd, cnew, cols, rate_cols,
+    send_r, send_l, col_send, corner_send, rxl, rxr, rx2, ry, rd, rd2, cnew, cols, rate_cols,
     ring, ring_send, ring_recv, means, mean_send, mean_recv,
     cols_new, wf_ref, wc_ref, rate8, edge_rate, shift_f, shift_c,
-    in_sem, send_sem, recv_sem,
+    in_sem, send_sem, recv_sem, ready_sem,
 ):
     F = fields
     fine_cols = frate.shape[2]
@@ -103,9 +110,11 @@
     below = lax.rem(gy + n_gy - 1, n_gy)
 
     barrier = pltpu.get_barrier_semaphore()
+    right2 = lax.rem(gx + 2, n_gx)
+    left2 = lax.rem(gx + n_gx - 2, n_gx)
     for target in (
-        (right, gy), (left, gy), (gx, above), (gx, below),
-        (right, above), (right, below), (left, above), (left, below),
+        (left, gy), (left, above), (left, below), (gx, above), (gx, below),
+        (left2, gy), (left2, above), (left2, below),
     ):
         pl.semaphore_signal(barrier, inc=1, device_id=target, device_id_type=MESH)
 
@@ -162,12 +171,17 @@
 
     load_coarse.wait()
     load_crate.wait()
-    for side, (x0, x1) in enumerate(((0, 1), (last, last - 1))):
+    first_row, first_rate = pl.ds(2 * F + 8, F), pl.ds(3 * F + 8, 8)
+    for side, buf, x0, x1 in ((0, send_l, 0, 1), (1, send_r, last, last - 1)):
         row, rate = old_row(x0), crate_row(x0)
-        row_send[side, near] = row
-        row_send[side, far] = old_row(x1)
-        row_send[side, rate_rows] = rate
+        buf[near] = row
+        buf[far] = old_row(x1)
+        buf[rate_rows] = rate
         pieces = [row[8 * j : 8 * j + 8] for j in range(F // 8)] + [rate]
+        if side:
+            buf[first_row] = old_row(0)
+            buf[first_rate] = crate_row(0)
+            pieces.append(crate_row(0))
         corner = pieces[0]
         for j, piece in enumerate(pieces):
             if j:
@@ -194,20 +208,20 @@
     keep_coarse = 0.75 - 6.0 * kappa
 
     pl.semaphore_wait(barrier, 8)
-    to_right = [
-        send(0, row_send.at[1], rx.at[0], (right, gy)),
-        send(4, corner_send.at[1], rd.at[0], (right, above)),
-        send(5, corner_send.at[1], rd.at[1], (right, below)),
-    ]
     to_side = [
         send(2, col_send.at[1], ry.at[0], (gx, above)),
         send(3, col_send.at[0], ry.at[1], (gx, below)),
     ]
-    to_left = [
-        send(1, row_send.at[0], rx.at[1], (left, gy)),
-        send(6, corner_send.at[0], rd.at[2], (left, above)),
-        send(7, corner_send.at[0], rd.at[3], (left, below)),
+    to_right = [
+        send(0, send_r, rxl, (right, gy)),
+        send(4, corner_send.at[1], rd.at[0], (right, above)),
+        send(5, corner_send.at[1], rd.at[1], (right, below)),
+        send(14, send_r.at[pl.ds(0, 2 * F + 8)], rx2, (right2, gy)),
+        send(15, corner_send.at[1], rd2.at[0], (right2, above)),
+        send(16, corner_send.at[1], rd2.at[1], (right2, below)),
     ]
+    for target in ((right, gy), (right, above), (right, below)):
+        pl.semaphore_signal(ready_sem, inc=1, device_id=target, device_id_type=MESH)
     for n in range(4):
         cols[n] = pack(old_row, mid - 2 + n, lane)
     for n in range(2):
@@ -216,8 +230,7 @@
     def wide(rate):
         return jnp.concatenate([rate] * (F // 8), axis=0)
 
-    def from_corner(m, src, dst):
-        tile = rd[m]
+    def from_corner(tile, src, dst):
         return jnp.concatenate([turn(tile, dst - src - 8 * j) for j in range(F // 8)], axis=0)
 
     def coarse_tiles(tiles):
@@ -226,9 +239,10 @@
         values = []
         for n, (center, lo, hi, ghost_lo, ghost_hi, _) in enumerate(tiles):
             part = shifted[F * n : F * n + F]
-            edge = 0.0 if ghost_hi is None else jnp.where(lane >= 120, ghost_hi, 0.0)
-            edge = jnp.where(lane < 8, ghost_lo, edge)
-            lateral = (lo + hi) + (part[:, :128] + edge)
+            lateral = (lo + hi) + part[:, :128]
+            if ghost_lo is not None:
+                edge = jnp.where(lane >= 120, ghost_hi, 0.0)
+                lateral = lateral + jnp.where(lane < 8, ghost_lo, edge)
             values.append(keep_coarse * center + kappa * lateral + part[:, 128:])
         return values
 
@@ -241,21 +255,25 @@
     def row_tile(x):
         if x == -1:
             return (
-                rx[0, near], rx[0, far], old_row(0),
-                from_corner(0, 64, 0), from_corner(1, 0, 120), wide(rx[0, rate_rows]),
+                rxl[near], rxl[far], old_row(0),
+                from_corner(rd[0], 64, 0), from_corner(rd[1], 0, 120), wide(rxl[rate_rows]),
             )
         if x == size_x:
             return (
-                rx[1, near], old_row(last), rx[1, far],
-                from_corner(2, 64, 0), from_corner(3, 0, 120), wide(rx[1, rate_rows]),
+                rxr[near], old_row(last), rxr[far],
+                from_corner(rd[2], 64, 0), from_corner(rd[3], 0, 120), wide(rxr[rate_rows]),
             )
         return (
             old_row(x),
-            old_row(x - 1) if x else rx[0, near],
-            old_row(x + 1) if x < last else rx[1, near],
+            old_row(x - 1) if x else rxl[near],
+            old_row(x + 1) if x < last else rxr[near],
             turn(ry[0, near], -8 * x), turn(ry[1, near], 120 - 8 * x),
             crate[pl.ds(x, 1), :],
         )
+
+    def extended(row, lo, hi, at=None):
+        at = lane if at is None else at
+        return jnp.where(at < 8, lo, jnp.where(at >= 120, hi, row))
 
     def joined(lo, hi, half):
         if half == 0:
@@ -279,48 +297,53 @@
             value = jnp.where(parents[p] == k, tiles[p][side], value)
         return value
 
-    def send_ring(level, row_at, col_at):
-        tiles = ring_tiles(row_at, col_at)
+    def send_ring(level, low_row, high_row, col_at):
+        tiles = ring_tiles([low_row] * 4, col_at)
+        halves = []
         for k in range(2):
-            for side in range(2):
-                ring_send[level, k, side] = chosen(tiles, k + 2, side)
+            value = jnp.zeros((F, 128), F32)
+            for p in range(4):
+                row = low_row if p // 2 else high_row
+                row = row if p % 2 == k else turn(row, 64)
+                value = jnp.where(parents[p] == k + 2, row, value)
+            halves.append(value)
+            ring_send[level, 1 + k] = chosen(tiles, k + 2, 1)
+        ring_send[level, 0] = jnp.where(first_half, halves[0], halves[1])
         return send(8 + level, ring_send.at[level], ring_recv.at[level], (right, gy))
 
-    corner_lanes = (lane // 8 == 7) | (lane // 8 == 15)
-
-    def end_share(share):
-        return (
-            jnp.where(corner_lanes, turn(share, 56), 0.0), jnp.where(corner_lanes, share, 0.0)
-        )
-
-    for copy in to_right + to_side:
+    group = lane // 8
+
+    def end_shares(before, after):
+        at_first = (group == 0) | (group == 8)
+        at_last = (group == 7) | (group == 15)
+        return [
+            jnp.where(at_first, before, 0.0), jnp.where(at_first, turn(before, 72), 0.0),
+            jnp.where(at_last, turn(after, 56), 0.0), jnp.where(at_last, after, 0.0),
+        ]
+
+    for copy in to_side:
         copy.wait_recv()
     old_cols = [ry[0, near], cols[1], cols[2], ry[1, near]]
-    ring_old = send_ring(
-        0, [rx[0, near], old_row(mid - 1), old_row(mid), old_row(mid)], old_cols
-    )
+    ring_old = send_ring(0, old_row(mid - 1), old_row(mid), old_cols)
     tiles = [
-        row_tile(-1), row_tile(mid - 1), row_tile(mid), row_tile(0),
-        (ry[0, near], ry[0, far], col_send[0, near], from_corner(0, 64, 0), None,
-         wide(ry[0, rate_rows])),
-        (cols[1], cols[0], cols[2], turn(rx[0, near], -8 * (mid - 1)), None, wide(rate_cols[0])),
-        (cols[2], cols[1], cols[3], turn(rx[0, near], -8 * mid), None, wide(rate_cols[1])),
-        (ry[1, near], col_send[1, near], ry[1, far], from_corner(1, 0, 0), None,
-         wide(ry[1, rate_rows])),
+        row_tile(mid - 1), row_tile(mid),
+        (ry[0, near], ry[0, far], col_send[0, near], None, None, wide(ry[0, rate_rows])),
+        (cols[1], cols[0], cols[2], None, None, wide(rate_cols[0])),
+        (cols[2], cols[1], cols[3], None, None, wide(rate_cols[1])),
+        (ry[1, near], col_send[1, near], ry[1, far], None, None, wide(ry[1, rate_rows])),
     ]
-    values = coarse_tiles(tiles)
-    end = jnp.where(lane >= 120, turn(ry[1, near], 120), old_row(0))
-    values.append(kappa * jnp.where(lane < 8, ry[0, near], end))
-    end_rate = jnp.where(lane8 >= 120, turn(rd[1], 96), rx[0, rate_rows])
-    end_rate = jnp.where(lane8 < 8, turn(rd[0], 40), end_rate)
-    result = react(values, [tile[5] for tile in tiles] + [wide(end_rate)])
-    new_before, new_cols = result[0], result[4:8]
-    cnew[mid - 1], cnew[mid], cnew[0] = result[1:4]
-    ring_new = send_ring(1, [new_before, result[1], result[2], result[2]], new_cols)
-    far_share = result[8]
-    for n, value in enumerate([new_before] + new_cols):
-        cols_new[n] = value
-    cols_new[5] = far_share
+    result = react(coarse_tiles(tiles), [tile[5] for tile in tiles])
+    cnew[mid - 1], cnew[mid] = result[:2]
+    for n in range(4):
+        cols_new[n] = result[2 + n]
+    ring_new = send_ring(1, result[0], result[1], result[2:])
+
+    pl.semaphore_wait(ready_sem, 3)
+    to_left = [
+        send(1, send_l, rxr, (left, gy)),
+        send(6, corner_send.at[0], rd.at[2], (left, above)),
+        send(7, corner_send.at[0], rd.at[3], (left, below)),
+    ]
 
     z16 = lane % 16
     row_index = (lane // 32) * 8 + z16 // 2
@@ -332,67 +355,108 @@
 
     load_frate.wait()
 
+    chunk = 8
+
     def spread_rate(s):
         for x in range(size_x):
             rate8[s, x] = jnp.broadcast_to(frate[s, pl.ds(x, 1), :], rate8.shape[2:])
 
-    def fine_step(s, step, edges, done=None):
+    def fine_jobs(s, step, get_edges, done=None):
+        state = {}
+
+        def edges_of():
+            if "edges" not in state:
+                state["edges"] = get_edges() if get_edges else None
+            return state["edges"]
+
         def row_of(x, h):
             if 0 <= x < size_x:
                 if step == 0:
                     return fin[s, h, pl.ds(x, F, stride=size_x), :]
                 return buf_b[s, x, :, pl.ds(h * 128, 128)]
+            edges = edges_of()
             if edges is None:
-                return jnp.zeros((F, 128), F32)
+                return None
             return pick(edges[0], row_index + 32 * h + (64 if x > 0 else 0))
 
-        weights = wf_ref[...]
-        live = jnp.full((F, 128), parent_ref[s], jnp.int32) >= 0
-        size = size_x // 2
-        for i in range(2):
-            rows = [[row_of(x, h) for h in range(2)] for x in range(size * i - 1, size * i + size + 1)]
-            shifted = shifted_sums(
+        def shift_part(i):
+            span = range(chunk * i - 1, chunk * i + chunk + 1)
+            rows = [[row_of(x, h) for h in range(2)] for x in span]
+            state[i] = rows, shifted_sums(
                 shift_f[...], jnp.concatenate([v for row in rows[1:-1] for v in row], axis=0)
             )
-            for m in range(size // 2):
-                j = size // 2 * i + m
-                if edges is None:
-                    ghost = 0.0
-                else:
-                    ghost = jnp.where(edge_lane, pick(edges[1], col_index + 8 * j), 0.0)
-                values, rates = [], []
+
+        def product_part(j):
+            edges = edges_of()
+            i, m = 2 * j // chunk, j % (chunk // 2)
+            rows, shifted = state[i]
+            if edges is None:
+                ghost = 0.0
+            else:
+                ghost = jnp.where(edge_lane, pick(edges[1], col_index + 8 * j), 0.0)
+            values = []
+            for n in range(2):
+                r = 2 * m + n + 1
+                v0, v1 = rows[r]
+                cross = [
+                    jnp.where(lane >= 112, turn(v1, 112), ghost),
+                    jnp.where(lane < 16, turn(v0, 16), ghost),
+                ]
+                for h in range(2):
+                    at = F * (2 * (r - 1) + h)
+                    part = shifted[at : at + F]
+                    lateral = part[:, :128] + cross[h]
+                    for near_row in (rows[r - 1][h], rows[r + 1][h]):
+                        if near_row is not None:
+                            lateral = lateral + near_row
+                    values.append(keep_fine * rows[r][h] + kappa2 * lateral + part[:, 128:])
+            state["p", j] = values, chemistry_product(wf_ref[...], values)
+
+        def sum_part(j):
+            values, product = state.pop(("p", j))
+            rates = [
+                wide(rate8[s, 2 * j + n, :, pl.ds(h * 128, 128)])
+                for n in range(2) for h in range(2)
+            ]
+            new = chemistry_sum(product, values, rates, F)
+            if step == 0:
                 for n in range(2):
-                    r = 2 * m + n + 1
-                    v0, v1 = rows[r]
-                    cross = [
-                        jnp.where(lane >= 112, turn(v1, 112), ghost),
-                        jnp.where(lane < 16, turn(v0, 16), ghost),
-                    ]
                     for h in range(2):
-                        at = F * (2 * (r - 1) + h)
-                        part = shifted[at : at + F]
-                        lateral = (part[:, :128] + cross[h]) + (rows[r - 1][h] + rows[r + 1][h])
-                        values.append(keep_fine * rows[r][h] + kappa2 * lateral + part[:, 128:])
-                        rates.append(wide(rate8[s, 2 * j + n, :, pl.ds(h * 128, 128)]))
-                new = chemistry(weights, values, rates, F)
-                if step == 0:
-                    for n in range(2):
-                        for h in range(2):
-                            buf_b[s, 2 * j + n, :, pl.ds(h * 128, 128)] = new[2 * n + h]
-                else:
-                    new = [jnp.where(live, v, 0.0) for v in new]
-                    for n in range(2):
-                        for h in range(2):
-                            fout[s, h, pl.ds(2 * j + n, F, stride=size_x), :] = new[2 * n + h]
-                    picked = []
+                        buf_b[s, 2 * j + n, :, pl.ds(h * 128, 128)] = new[2 * n + h]
+            else:
+                live = jnp.full((F, 128), parent_ref[s], jnp.int32) >= 0
+                new = [jnp.where(live, v, 0.0) for v in new]
+                for n in range(2):
                     for h in range(2):
-                        total = new[h] + new[2 + h]
-                        total = total + turn(total, 127)
-                        total = total + turn(total, 112)
-                        picked.append(pick(total, mean_index))
-                    means[s, j] = 0.125 * jnp.where(mean_low, picked[0], picked[1])
+                        fout[s, h, pl.ds(2 * j + n, F, stride=size_x), :] = new[2 * n + h]
+                picked = []
+                for h in range(2):
+                    total = new[h] + new[2 + h]
+                    total = total + turn(total, 127)
+                    total = total + turn(total, 112)
+                    picked.append(pick(total, mean_index))
+                means[s, j] = 0.125 * jnp.where(mean_low, picked[0], picked[1])
             if done is not None:
-                done(i)
+                done(j)
+
+        pairs = size_x // 2
+        return [
+            (
+                functools.partial(shift_part, 2 * j // chunk) if 2 * j % chunk == 0 else None,
+                functools.partial(product_part, j), functools.partial(sum_part, j),
+            )
+            for j in range(pairs)
+        ]
+
+    def run(jobs):
+        lead, lag = 4, 2
+        for n in range(-lead, len(jobs) + lag):
+            if n + lead < len(jobs) and jobs[n + lead][0] is not None:
+                jobs[n + lead][0]()
+            if 0 <= n < len(jobs):
+                jobs[n][1]()
+            if n >= lag:
+                jobs[n - lag][2]()
 
     def pack_edge_rate(s):
         for q in range(size_x // 4):
@@ -402,7 +466,7 @@
                 hi = turn(rate8[s, 4 * q + n, :, pl.ds(fine_cols - 128, 128)], 16 * n - 48)
                 total = jnp.where(lane8 // 16 == n, lo, total)
                 total = jnp.where(lane8 // 16 == 4 + n, hi, total)
-            edge_rate[s - 2, q] = total
+            edge_rate[s, q] = total
 
     edge_index = (lane // 64) * 64 + ((lane % 64) // 32) * 8 + z16 // 2
 
@@ -415,7 +479,7 @@
                 rates.append(wide(rate8[s, x, :, pl.ds(h * 128, 128)]))
         for q in range(size_x // 4):
             values.append(kappa2 * pick(edge_y, edge_index + 16 * q))
-            rates.append(wide(edge_rate[s - 2, q]))
+            rates.append(wide(edge_rate[s, q]))
         share = chemistry(wf_ref[...], values, rates, F)
         for x in range(size_x):
             q, n = x // 4, x % 4
@@ -435,41 +499,124 @@
     def mid_edges(s):
         return [0.5 * (ring[0, s, side] + ring[1, s, side]) for side in range(2)]
 
-    for s in (2, 3):
+    for s in order:
         for copy in fine_loads[s]:
             copy.wait()
+    for s in order:
         spread_rate(s)
         pack_edge_rate(s)
-        fine_step(s, 0, None)
+    run([job for s in order for job in fine_jobs(s, 0, None)])
 
     homes = [jnp.full((F, 128), parent_ref[s], jnp.int32) for s in range(slots)]
 
-    def take_ring(level, row):
-        turned = turn(row, 64)
+    def fill_rows(rows):
+        for at in range(0, len(rows), 4):
+            tiles = [row_tile(x) for x in rows[at : at + 4]]
+            result = react(coarse_tiles(tiles), [tile[5] for tile in tiles])
+            for x, value in zip(rows[at : at + 4], result):
+                cnew[x] = value
+
+    fill_rows([x for x in range(1, last) if x not in (mid - 1, mid)])
+
+    for copy in to_right:
+        copy.wait_recv()
+    tiles = [
+        row_tile(-1), row_tile(0),
+        (
+            rx2[near], rx2[far], rxl[first_row],
+            from_corner(rd2[0], 64, 0), from_corner(rd2[1], 0, 120), wide(rx2[rate_rows]),
+        ),
+    ]
+    values = coarse_tiles(tiles)
+    rates = [tile[5] for tile in tiles]
+    values.append(
+        kappa * extended(old_row(0), ry[0, near], turn(ry[1, near], 120))
+    )
+    rates.append(wide(extended(rxl[rate_rows], turn(rd[0], 40), turn(rd[1], 96), lane8)))
+    values.append(kappa * extended(rx2[near], tiles[2][3], tiles[2][4]))
+    rates.append(wide(extended(rxl[first_rate], turn(rd[0], 32), turn(rd[1], 88), lane8)))
+    values.append(kappa * extended(rxl[near], tiles[0][3], tiles[0][4]))
+    rates.append(
+        wide(extended(crate_row(0), ry[0, rate_rows], turn(ry[1, rate_rows], 120), lane8))
+    )
+    result = react(values, rates)
+    cnew[0] = result[1]
+    for n, value in zip(range(4, 9), (result[0], result[2], result[3], result[4], result[5])):
+        cols_new[n] = value
+
+    def take_ring(level):
+        before = cols_new[5] if level else rx2[near]
+        after = cnew[0] if level else old_row(0)
+        fix = end_shares(cols_new[7], cols_new[6]) if level else None
+        shared = ring_recv[level, 0]
+        turned = turn(shared, 64)
         for k in range(2):
             home = homes[k + 2]
-            value = ring_recv[level, k, 0]
-            value = jnp.where((home == 2) & ~first_half, turned, value)
-            value = jnp.where((home == 3) & ~first_half, row, value)
+            low, high = (shared, turned) if k == 0 else (turned, shared)
+            kinds = [
+                jnp.where(first_half, before, high), jnp.where(first_half, turn(before, 64), high),
+                jnp.where(first_half, low, turn(after, 64)), jnp.where(first_half, low, after),
+            ]
+            value, added = kinds[3], fix[3] if level else None
+            for p in range(3):
+                value = jnp.where(home == p, kinds[p], value)
+                if level:
+                    added = jnp.where(home == p, fix[p], added)
             ring[level, k + 2, 0] = value
-            value = ring_recv[level, k, 1]
-            if level:
-                fix = end_share(cols_new[5])
-                added = jnp.where(home == 2, fix[0], jnp.where(home == 3, fix[1], 0.0))
-                value = value + added
-            ring[level, k + 2, 1] = value
+            value = ring_recv[level, 1 + k]
+            ring[level, k + 2, 1] = value + added if level else value
+
+    def local_part():
+        for copy in to_left:
+            copy.wait_recv()
+        tiles = [row_tile(last), row_tile(size_x)]
+        values = coarse_tiles(tiles)
+        values.append(
+            kappa * extended(rxr[near], from_corner(rd[2], 64, 0), from_corner(rd[3], 0, 120))
+        )
+        rate = extended(crate_row(last), turn(ry[0, rate_rows], 8), ry[1, rate_rows], lane8)
+        result = react(values, [tile[5] for tile in tiles] + [wide(rate)])
+        cnew[last] = result[0]
+        fix = end_shares(cols_new[8], result[2])
+        tiles_old = ring_tiles(
+            [rxl[near], old_row(mid - 1), old_row(mid), rxr[near]],
+            [ry[0, near], cols[1], cols[2], ry[1, near]],
+        )
+        tiles_new = ring_tiles(
+            [cols_new[4], cnew[mid - 1], cnew[mid], result[1]], [cols_new[n] for n in range(4)]
+        )
+        tiles_new = [(tile[0], tile[1] + fix[p]) for p, tile in enumerate(tiles_new)]
+        for k in range(2):
+            for side in range(2):
+                ring[0, k, side] = chosen(tiles_old, k, side)
+                ring[1, k, side] = chosen(tiles_new, k, side)
+        for s in (0, 1):
+            correct(s)
+        run(
+            [
+                job for s in (0, 1)
+                for job in fine_jobs(s, 1, functools.partial(mid_edges, s))
+            ]
+        )
+
+    @pl.when(gx == 0)
+    def _():
+        local_part()
 
     ring_old.wait_recv()
-    take_ring(0, old_row(0))
+    take_ring(0)
     for s in (2, 3):
         correct(s)
     ring_new.wait_recv()
-    take_ring(1, cnew[0])
-
-    sent = []
+    take_ring(1)
+
+    sent, jobs = [], []
     for s in (2, 3):
         def send_part(i, s=s):
             size = size_x // 8
+            if 4 * (i + 1) % size_x:
+                return
+            i = 4 * i // size_x
             for m in range(size):
                 j = 2 * (size * i + m)
                 mean_send[s - 2, i, m] = jnp.where(first_half, means[s, j], means[s, j + 1])
@@ -479,41 +626,13 @@
                 )
             )
 
-        fine_step(s, 1, mid_edges(s), send_part)
-
-    for copy in to_left:
-        copy.wait_recv()
-    rest = [x for x in range(1, size_x + 1) if x not in (mid - 1, mid)]
-    values, rates = [], []
-    for at in range(0, len(rest), 2):
-        tiles = [row_tile(x) for x in rest[at : at + 2]]
-        values += coarse_tiles(tiles)
-        rates += [tile[5] for tile in tiles]
-    end = jnp.where(lane < 8, from_corner(2, 64, 0), rx[1, near])
-    values.append(kappa * jnp.where(lane >= 120, from_corner(3, 0, 120), end))
-    end_rate = jnp.where(lane8 < 8, turn(ry[0, rate_rows], 8), crate_row(last))
-    rates.append(wide(jnp.where(lane8 >= 120, ry[1, rate_rows], end_rate)))
-    result = react(values, rates)
-    for x, value in zip(rest[:-1], result):
-        cnew[x] = value
-    fix = end_share(result[-1])
-    tiles_old = ring_tiles([rx[0, near], old_row(mid - 1), old_row(mid), rx[1, near]], old_cols)
-    tiles_new = ring_tiles(
-        [cols_new[0], cnew[mid - 1], cnew[mid], result[-2]], [cols_new[n] for n in range(1, 5)]
-    )
-    for p in (2, 3):
-        tiles_new[p] = (tiles_new[p][0], tiles_new[p][1] + fix[p - 2])
-    for k in range(2):
-        for side in range(2):
-            ring[0, k, side] = chosen(tiles_old, k, side)
-            ring[1, k, side] = chosen(tiles_new, k, side)
-
-    for s in (0, 1):
-        for copy in fine_loads[s]:
-            copy.wait()
-        spread_rate(s)
-        fine_step(s, 0, [ring[0, s, 0], ring[0, s, 1]])
-        fine_step(s, 1, mid_edges(s))
+        jobs += fine_jobs(s, 1, functools.partial(mid_edges, s), send_part)
+    run(jobs)
+
+    @pl.when(gx != 0)
+    def _():
+        local_part()
+
     for copy in sent:
         copy.wait_recv()
 
@@ -577,31 +696,36 @@
             V((slots, 2, flat, 128), F32),
             V((slots, size_x, fine_merged), F32),
             V((slots, size_x, fields, fine_merged), F32),
-            V((2, 2 * fields + 8, 128), F32),
+            V((3 * fields + 16, 128), F32),
+            V((2 * fields + 8, 128), F32),
             V((2, 2 * fields + 8, 128), F32),
             V((2, 8, 128), F32),
-            V((2, 2 * fields + 8, 128), F32),
+            V((3 * fields + 16, 128), F32),
+            V((2 * fields + 8, 128), F32),
+            V((2 * fields + 8, 128), F32),
             V((2, 2 * fields + 8, 128), F32),
             V((4, 8, 128), F32),
+            V((2, 8, 128), F32),
             V((size_x,) + tile, F32),
             V((4,) + tile, F32),
             V((2, 8, 128), F32),
             V((2, slots, 2) + tile, F32),
-            V((2, 2, 2) + tile, F32),
-            V((2, 2, 2) + tile, F32),
+            V((2, 3) + tile, F32),
+            V((2, 3) + tile, F32),
             V((slots, size_x // 2) + tile, F32),
             V((2, 2, size_x // 8) + tile, F32),
             V((2, 2, size_x // 8) + tile, F32),
-            V((6,) + tile, F32),
+            V((9,) + tile, F32),
             V((4 * fields, 3 * fields), BF16),
             V((4 * fields, 3 * fields), BF16),
             V((slots, size_x, 8, fine_merged), F32),
-            V((2, size_x // 4, 8, 128), F32),
+            V((slots, size_x // 4, 8, 128), F32),
             V((256, 256), BF16),
             V((256, 256), BF16),
             pltpu.SemaphoreType.DMA((15,)),
-            pltpu.SemaphoreType.DMA((14,)),
-            pltpu.SemaphoreType.DMA((14,)),
+            pltpu.SemaphoreType.DMA((17,)),
+            pltpu.SemaphoreType.DMA((17,)),
+            pltpu.SemaphoreType.REGULAR,
         ],
         compiler_params=pltpu.CompilerParams(
             collective_id=0, has_side_effects=True, vmem_limit_bytes=24 * 2**20

time: 23.3 us -> 20.4 us (0.88)
  Pallas kernels: 22.5 us -> 19.6 us
    pallas_call x1, Pallas kernels: 21.3 us -> 18.3 us  [body(): pl.pallas_call(functools.partial(kernel, lax.axis_size('gx'), lax.axis_si...]
where the time goes in v3:
time: 20.4 us; the launch traced here: 20.2 us
  Pallas kernels  19.6 us (96%)
  between operations  0.64 us (3%)
    pallas_call x1, Pallas kernels, body(): pl.pallas_call(functools.partial(kernel, lax.axis_size('gx'), lax.axis_si...  18.3 us
    pallas_call x1, Pallas kernels, body(): pl.pallas_call(store_kernel, out_shape=(jax.ShapeDtypeStruct((flat, merge...  1.27 us

profile of v3, /device:TPU:0, one launch (start us, length us, event | category | flops | bytes accessed | tf_op | source)
XLA Modules:
  0.0 20.2 jit_solution(478808729204499499)
XLA Ops:
  0.6 18.3 %shard_map.95 = (f32[384,128]{1,0:T(8,128)S(1)}, f32[4,2,384,128]{3,2,1,0:T(8,128)S(1)}) custom-call(s32[4]{0:T(128)} %refine_hbm.1, s32[4]{0:T(128)} %parent_hbm.1, f32[384,128]{1,0:T(8,128)} %bitcast.6, f32[16,128]{1,0:T(8,128)} %crate_hbm.1, f32[4,384,256]{2,1,0:T(8,128)} %bitcast.5, f32[4,16,256]{2,1,0:T(8,128)} %frate_hbm.1, f32[1,24]{1,0:T(1,128)} %bitcast.7, ...), custom_call_target="tpu_custom_call" | custom-call | tf_op jit(solution)/shard_map/pallas_call | solution.py:682
  19.0 1.3 %shard_map.96 = (f32[384,128]{1,0:T(8,128)}, f32[4,384,256]{2,1,0:T(8,128)}) custom-call(f32[384,128]{1,0:T(8,128)S(1)} %get-tuple-element.6.cout, f32[4,2,384,128]{3,2,1,0:T(8,128)S(1)} %get-tuple-element.7.fout), custom_call_target="tpu_custom_call" | custom-call | tf_op jit(solution)/shard_map/pallas_call | solution.py:743

commit v4 on v3

--- a/solution.py
+++ b/solution.py
@@ -112,10 +112,9 @@
     barrier = pltpu.get_barrier_semaphore()
     right2 = lax.rem(gx + 2, n_gx)
     left2 = lax.rem(gx + n_gx - 2, n_gx)
-    for target in (
-        (left, gy), (left, above), (left, below), (gx, above), (gx, below),
-        (left2, gy), (left2, above), (left2, below),
-    ):
+    sides = [above] if n_gy == 2 else [above, below]
+    targets = [(x, y) for x in (left, left2) for y in [gy] + sides] + [(gx, y) for y in sides]
+    for target in targets:
         pl.semaphore_signal(barrier, inc=1, device_id=target, device_id_type=MESH)
 
     load_coarse = pltpu.make_async_copy(coarse_hbm, cin, in_sem.at[0])
@@ -155,16 +154,6 @@
     lane8 = lanes(8)
     first_half = lane < 64
 
-    shift_f[...] = shift_matrix(16)
-    shift_c[...] = shift_matrix(8)
-
-    def pack(rows_of, y, at):
-        total = None
-        for x in range(size_x):
-            moved = turn(rows_of(x), (x - y) * 8)
-            total = moved if total is None else jnp.where(at // 8 == x, moved, total)
-        return total
-
     near, far, rate_rows = pl.ds(0, F), pl.ds(F, F), pl.ds(2 * F, 8)
     old_row = lambda x: cin[pl.ds(x, F, stride=size_x), :]
     crate_row = lambda x: jnp.broadcast_to(crate[pl.ds(x, 1), :], (8, 128))
@@ -172,7 +161,7 @@
     load_coarse.wait()
     load_crate.wait()
     first_row, first_rate = pl.ds(2 * F + 8, F), pl.ds(3 * F + 8, 8)
-    for side, buf, x0, x1 in ((0, send_l, 0, 1), (1, send_r, last, last - 1)):
+    def fill_row_message(side, buf, x0, x1):
         row, rate = old_row(x0), crate_row(x0)
         buf[near] = row
         buf[far] = old_row(x1)
@@ -188,10 +177,50 @@
                 corner = jnp.where(lane8 // 8 == j, turn(piece, 8 * j), corner)
             corner = jnp.where(lane8 // 8 == 8 + j, turn(piece, 8 * j - 56), corner)
         corner_send[side] = corner
+    fill_row_message(1, send_r, last, last - 1)
+    pl.semaphore_wait(barrier, len(targets))
+    to_right = [
+        send(0, send_r, rxl, (right, gy)),
+        send(14, send_r.at[pl.ds(0, 2 * F + 8)], rx2, (right2, gy)),
+    ]
+    to_right1, to_right2 = to_right[:1], to_right[1:]
+    for n, y in enumerate(sides):
+        to_right1.append(send(4 + n, corner_send.at[1], rd.at[n], (right, y)))
+        to_right2.append(send(15 + n, corner_send.at[1], rd2.at[n], (right2, y)))
+    to_right = to_right1 + to_right2
+    for y in [gy] + sides:
+        pl.semaphore_signal(ready_sem, inc=1, device_id=(right, y), device_id_type=MESH)
+
+    group32 = lanes(F + 8) // 8
+    columns = {
+        x: jnp.concatenate([old_row(x), crate_row(x)], axis=0) for x in range(size_x)
+    }
+    wanted = (0, 1, mid - 2, mid - 1, mid, mid + 1, last - 1, last)
+    bits = [size_x // 8, size_x // 4, 1, size_x // 2]
+    for n, bit in enumerate(bits):
+        free = sum(bits[n + 1 :])
+        moved = {}
+        for x in range(size_x):
+            if any((x ^ y) & ~free == 0 for y in wanted):
+                other = columns[x ^ bit]
+                lower = group32 & bit == 0
+                if x & bit:
+                    moved[x] = jnp.where(lower, turn(other, -8 * bit), columns[x])
+                else:
+                    moved[x] = jnp.where(lower, columns[x], turn(other, 8 * bit))
+        columns = moved
     for side, (y0, y1) in enumerate(((0, 1), (last, last - 1))):
-        col_send[side, near] = pack(old_row, y0, lane)
-        col_send[side, far] = pack(old_row, y1, lane)
-        col_send[side, rate_rows] = pack(crate_row, y0, lane8)
+        col_send[side, near] = columns[y0][:F]
+        col_send[side, far] = columns[y1][:F]
+        col_send[side, rate_rows] = columns[y0][F:]
+    to_side = [
+        send(2, col_send.at[1], ry.at[0], (gx, above)),
+        send(3, col_send.at[0], ry.at[1], (gx, below)),
+    ]
+    for n in range(4):
+        cols[n] = columns[mid - 2 + n][:F]
+    for n in range(2):
+        rate_cols[n] = columns[mid - 1 + n][F:]
 
     for copy in small:
         copy.wait()
@@ -206,26 +235,10 @@
     kappa2 = 2.0 * kappa
     keep_fine = 0.75 - 6.0 * kappa2
     keep_coarse = 0.75 - 6.0 * kappa
-
-    pl.semaphore_wait(barrier, 8)
-    to_side = [
-        send(2, col_send.at[1], ry.at[0], (gx, above)),
-        send(3, col_send.at[0], ry.at[1], (gx, below)),
-    ]
-    to_right = [
-        send(0, send_r, rxl, (right, gy)),
-        send(4, corner_send.at[1], rd.at[0], (right, above)),
-        send(5, corner_send.at[1], rd.at[1], (right, below)),
-        send(14, send_r.at[pl.ds(0, 2 * F + 8)], rx2, (right2, gy)),
-        send(15, corner_send.at[1], rd2.at[0], (right2, above)),
-        send(16, corner_send.at[1], rd2.at[1], (right2, below)),
-    ]
-    for target in ((right, gy), (right, above), (right, below)):
-        pl.semaphore_signal(ready_sem, inc=1, device_id=target, device_id_type=MESH)
-    for n in range(4):
-        cols[n] = pack(old_row, mid - 2 + n, lane)
-    for n in range(2):
-        rate_cols[n] = pack(crate_row, mid - 1 + n, lane8)
+    shift_c[...] = shift_matrix(8)
+    fill_row_message(0, send_l, 0, 1)
+    corners = [rd.at[n] for n in ((0, 0, 2, 2) if n_gy == 2 else (0, 1, 2, 3))]
+    corners2 = [rd2.at[n] for n in ((0, 0) if n_gy == 2 else (0, 1))]
 
     def wide(rate):
         return jnp.concatenate([rate] * (F // 8), axis=0)
@@ -256,12 +269,12 @@
         if x == -1:
             return (
                 rxl[near], rxl[far], old_row(0),
-                from_corner(rd[0], 64, 0), from_corner(rd[1], 0, 120), wide(rxl[rate_rows]),
+                from_corner(corners[0][...], 64, 0), from_corner(corners[1][...], 0, 120), wide(rxl[rate_rows]),
             )
         if x == size_x:
             return (
                 rxr[near], old_row(last), rxr[far],
-                from_corner(rd[2], 64, 0), from_corner(rd[3], 0, 120), wide(rxr[rate_rows]),
+                from_corner(corners[2][...], 64, 0), from_corner(corners[3][...], 0, 120), wide(rxr[rate_rows]),
             )
         return (
             old_row(x),
@@ -338,13 +351,7 @@
         cols_new[n] = result[2 + n]
     ring_new = send_ring(1, result[0], result[1], result[2:])
 
-    pl.semaphore_wait(ready_sem, 3)
-    to_left = [
-        send(1, send_l, rxr, (left, gy)),
-        send(6, corner_send.at[0], rd.at[2], (left, above)),
-        send(7, corner_send.at[0], rd.at[3], (left, below)),
-    ]
-
+    shift_f[...] = shift_matrix(16)
     z16 = lane % 16
     row_index = (lane // 32) * 8 + z16 // 2
     col_index = jnp.where(lane < 64, 0, 64) + z16 // 2
@@ -470,7 +477,7 @@
 
     edge_index = (lane // 64) * 64 + ((lane % 64) // 32) * 8 + z16 // 2
 
-    def correct(s):
+    def correction(s):
         edge_x, edge_y = ring[0, s, 0], ring[0, s, 1]
         values, rates = [], []
         for side, x in ((0, 0), (1, last)):
@@ -480,7 +487,14 @@
         for q in range(size_x // 4):
             values.append(kappa2 * pick(edge_y, edge_index + 16 * q))
             rates.append(wide(edge_rate[s, q]))
-        share = chemistry(wf_ref[...], values, rates, F)
+        return chemistry(wf_ref[...], values, rates, F)
+
+    def correct(slot_list):
+        shares = [correction(s) for s in slot_list]
+        for s, share in zip(slot_list, shares):
+            add_correction(s, share)
+
+    def add_correction(s, share):
         for x in range(size_x):
             q, n = x // 4, x % 4
             both = share[4 + q]
@@ -518,31 +532,57 @@
 
     fill_rows([x for x in range(1, last) if x not in (mid - 1, mid)])
 
-    for copy in to_right:
+    pl.semaphore_wait(ready_sem, 1 + len(sides))
+    to_left = [send(1, send_l, rxr, (left, gy))]
+    for n, y in enumerate(sides):
+        to_left.append(send(6 + n, corner_send.at[0], rd.at[2 + n], (left, y)))
+
+    for copy in to_right1:
         copy.wait_recv()
-    tiles = [
-        row_tile(-1), row_tile(0),
-        (
-            rx2[near], rx2[far], rxl[first_row],
-            from_corner(rd2[0], 64, 0), from_corner(rd2[1], 0, 120), wide(rx2[rate_rows]),
-        ),
-    ]
+    tiles = [row_tile(-1), row_tile(0)]
     values = coarse_tiles(tiles)
     rates = [tile[5] for tile in tiles]
     values.append(
         kappa * extended(old_row(0), ry[0, near], turn(ry[1, near], 120))
     )
-    rates.append(wide(extended(rxl[rate_rows], turn(rd[0], 40), turn(rd[1], 96), lane8)))
-    values.append(kappa * extended(rx2[near], tiles[2][3], tiles[2][4]))
-    rates.append(wide(extended(rxl[first_rate], turn(rd[0], 32), turn(rd[1], 88), lane8)))
+    rates.append(
+        wide(
+            extended(
+                rxl[rate_rows], turn(corners[0][...], 40), turn(corners[1][...], 96), lane8
+            )
+        )
+    )
     values.append(kappa * extended(rxl[near], tiles[0][3], tiles[0][4]))
     rates.append(
         wide(extended(crate_row(0), ry[0, rate_rows], turn(ry[1, rate_rows], 120), lane8))
     )
     result = react(values, rates)
     cnew[0] = result[1]
-    for n, value in zip(range(4, 9), (result[0], result[2], result[3], result[4], result[5])):
+    for n, value in zip((4, 6, 8), (result[0], result[2], result[3])):
         cols_new[n] = value
+
+    def far_rows():
+        for copy in to_right2:
+            copy.wait_recv()
+        tiles = [
+            (
+                rx2[near], rx2[far], rxl[first_row],
+                from_corner(corners2[0][...], 64, 0), from_corner(corners2[1][...], 0, 120), wide(rx2[rate_rows]),
+            ),
+        ]
+        values = coarse_tiles(tiles)
+        rates = [tile[5] for tile in tiles]
+        values.append(kappa * extended(rx2[near], tiles[0][3], tiles[0][4]))
+        rates.append(
+            wide(
+                extended(
+                    rxl[first_rate], turn(corners[0][...], 32), turn(corners[1][...], 88), lane8
+                )
+            )
+        )
+        result = react(values, rates)
+        cols_new[5] = result[0]
+        cols_new[7] = result[1]
 
     def take_ring(level):
         before = cols_new[5] if level else rx2[near]
@@ -566,13 +606,13 @@
             value = ring_recv[level, 1 + k]
             ring[level, k + 2, 1] = value + added if level else value
 
-    def local_part():
+    def local_rings():
         for copy in to_left:
             copy.wait_recv()
         tiles = [row_tile(last), row_tile(size_x)]
         values = coarse_tiles(tiles)
         values.append(
-            kappa * extended(rxr[near], from_corner(rd[2], 64, 0), from_corner(rd[3], 0, 120))
+            kappa * extended(rxr[near], from_corner(corners[2][...], 64, 0), from_corner(corners[3][...], 0, 120))
         )
         rate = extended(crate_row(last), turn(ry[0, rate_rows], 8), ry[1, rate_rows], lane8)
         result = react(values, [tile[5] for tile in tiles] + [wide(rate)])
@@ -590,33 +630,41 @@
             for side in range(2):
                 ring[0, k, side] = chosen(tiles_old, k, side)
                 ring[1, k, side] = chosen(tiles_new, k, side)
-        for s in (0, 1):
-            correct(s)
+
+    def local_steps(slot_list):
+        correct(slot_list)
         run(
             [
-                job for s in (0, 1)
+                job for s in slot_list
                 for job in fine_jobs(s, 1, functools.partial(mid_edges, s))
             ]
         )
 
     @pl.when(gx == 0)
     def _():
-        local_part()
-
+        local_rings()
+        local_steps((0,))
+
+    far_rows()
     ring_old.wait_recv()
     take_ring(0)
-    for s in (2, 3):
-        correct(s)
+    correct((2, 3))
     ring_new.wait_recv()
     take_ring(1)
 
     sent, jobs = [], []
     for s in (2, 3):
         def send_part(i, s=s):
-            size = size_x // 8
             if 4 * (i + 1) % size_x:
                 return
             i = 4 * i // size_x
+            if s == 2 and i == 0:
+                return
+            for i in (0, 1) if s == 2 else (i,):
+                send_half(i, s)
+
+        def send_half(i, s):
+            size = size_x // 8
             for m in range(size):
                 j = 2 * (size * i + m)
                 mean_send[s - 2, i, m] = jnp.where(first_half, means[s, j], means[s, j + 1])
@@ -629,9 +677,14 @@
         jobs += fine_jobs(s, 1, functools.partial(mid_edges, s), send_part)
     run(jobs)
 
+    @pl.when(gx == 0)
+    def _():
+        local_steps((1,))
+
     @pl.when(gx != 0)
     def _():
-        local_part()
+        local_rings()
+        local_steps((0, 1))
 
     for copy in sent:
         copy.wait_recv()

time: 20.4 us -> 19.2 us (0.941)
  Pallas kernels: 19.6 us -> 18.4 us
    pallas_call x1, Pallas kernels: 18.3 us -> 17.1 us  [body(): pl.pallas_call(functools.partial(kernel, lax.axis_size('gx'), lax.axis_si...]
where the time goes in v4:
time: 19.2 us; the launch traced here: 19 us
  Pallas kernels  18.4 us (96%)
  between operations  0.64 us (3%)
    pallas_call x1, Pallas kernels, body(): pl.pallas_call(functools.partial(kernel, lax.axis_size('gx'), lax.axis_si...  17.1 us
    pallas_call x1, Pallas kernels, body(): pl.pallas_call(store_kernel, out_shape=(jax.ShapeDtypeStruct((flat, merge...  1.27 us

profile of v4, /device:TPU:0, one launch (start us, length us, event | category | flops | bytes accessed | tf_op | source)
XLA Modules:
  0.0 19.0 jit_solution(14499903814809694030)
XLA Ops:
  0.6 17.1 %shard_map.95 = (f32[384,128]{1,0:T(8,128)S(1)}, f32[4,2,384,128]{3,2,1,0:T(8,128)S(1)}) custom-call(s32[4]{0:T(128)} %refine_hbm.1, s32[4]{0:T(128)} %parent_hbm.1, f32[384,128]{1,0:T(8,128)} %bitcast.6, f32[16,128]{1,0:T(8,128)} %crate_hbm.1, f32[4,384,256]{2,1,0:T(8,128)} %bitcast.5, f32[4,16,256]{2,1,0:T(8,128)} %frate_hbm.1, f32[1,24]{1,0:T(1,128)} %bitcast.7, ...), custom_call_target="tpu_custom_call" | custom-call | tf_op jit(solution)/shard_map/pallas_call | solution.py:735
  17.7 1.3 %shard_map.96 = (f32[384,128]{1,0:T(8,128)}, f32[4,384,256]{2,1,0:T(8,128)}) custom-call(f32[384,128]{1,0:T(8,128)S(1)} %get-tuple-element.6.cout, f32[4,2,384,128]{3,2,1,0:T(8,128)S(1)} %get-tuple-element.7.fout), custom_call_target="tpu_custom_call" | custom-call | tf_op jit(solution)/shard_map/pallas_call | solution.py:796

commit v5 on v4

--- a/solution.py
+++ b/solution.py
@@ -138,9 +138,6 @@
     order = (2, 3, 0, 1)
     for copy in [load_coarse, load_crate] + small + [load_frate]:
         copy.start()
-    for s in order:
-        for copy in fine_loads[s]:
-            copy.start()
 
     def send(n, src, dst, target):
         copy = pltpu.make_async_remote_copy(
@@ -160,6 +157,9 @@
 
     load_coarse.wait()
     load_crate.wait()
+    for s in order:
+        for copy in fine_loads[s]:
+            copy.start()
     first_row, first_rate = pl.ds(2 * F + 8, F), pl.ds(3 * F + 8, 8)
     def fill_row_message(side, buf, x0, x1):
         row, rate = old_row(x0), crate_row(x0)
@@ -632,7 +632,6 @@
                 ring[1, k, side] = chosen(tiles_new, k, side)
 
     def local_steps(slot_list):
-        correct(slot_list)
         run(
             [
                 job for s in slot_list
@@ -643,7 +642,7 @@
     @pl.when(gx == 0)
     def _():
         local_rings()
-        local_steps((0,))
+        correct((0, 1))
 
     far_rows()
     ring_old.wait_recv()
@@ -677,14 +676,12 @@
         jobs += fine_jobs(s, 1, functools.partial(mid_edges, s), send_part)
     run(jobs)
 
-    @pl.when(gx == 0)
-    def _():
-        local_steps((1,))
-
     @pl.when(gx != 0)
     def _():
         local_rings()
-        local_steps((0, 1))
+        correct((0, 1))
+
+    local_steps((0, 1))
 
     for copy in sent:
         copy.wait_recv()

time: 19.2 us -> 18.7 us (0.974)
  Pallas kernels: 18.4 us -> 17.9 us
    pallas_call x1, Pallas kernels: 17.1 us -> 16.6 us  [body(): pl.pallas_call(functools.partial(kernel, lax.axis_size('gx'), lax.axis_si...]
where the time goes in v5:
time: 18.7 us; the launch traced here: 18.5 us
  Pallas kernels  17.9 us (96%)
  between operations  0.64 us (3%)
    pallas_call x1, Pallas kernels, body(): pl.pallas_call(functools.partial(kernel, lax.axis_size('gx'), lax.axis_si...  16.6 us
    pallas_call x1, Pallas kernels, body(): pl.pallas_call(store_kernel, out_shape=(jax.ShapeDtypeStruct((flat, merge...  1.27 us

profile of v5, /device:TPU:0, one launch (start us, length us, event | category | flops | bytes accessed | tf_op | source)
XLA Modules:
  0.0 18.5 jit_solution(10688857033464243530)
XLA Ops:
  0.6 16.6 %shard_map.95 = (f32[384,128]{1,0:T(8,128)S(1)}, f32[4,2,384,128]{3,2,1,0:T(8,128)S(1)}) custom-call(s32[4]{0:T(128)} %refine_hbm.1, s32[4]{0:T(128)} %parent_hbm.1, f32[384,128]{1,0:T(8,128)} %bitcast.6, f32[16,128]{1,0:T(8,128)} %crate_hbm.1, f32[4,384,256]{2,1,0:T(8,128)} %bitcast.5, f32[4,16,256]{2,1,0:T(8,128)} %frate_hbm.1, f32[1,24]{1,0:T(1,128)} %bitcast.7, ...), custom_call_target="tpu_custom_call" | custom-call | tf_op jit(solution)/shard_map/pallas_call | solution.py:732
  17.2 1.3 %shard_map.96 = (f32[384,128]{1,0:T(8,128)}, f32[4,384,256]{2,1,0:T(8,128)}) custom-call(f32[384,128]{1,0:T(8,128)S(1)} %get-tuple-element.6.cout, f32[4,2,384,128]{3,2,1,0:T(8,128)S(1)} %get-tuple-element.7.fout), custom_call_target="tpu_custom_call" | custom-call | tf_op jit(solution)/shard_map/pallas_call | solution.py:793
